TPU v7x, 256 devices: a whole 4x4x8 slice. The times are simulated.
256 devices in a mesh: gz: 8 (over z), rows: 32 (over x, y, core).
Axes of the slice: x: 4, y: 4, z: 8, core: 2. Of those that a mesh axis runs over, the one named last changes fastest.
Arguments:
- sections: bfloat16 [1, 8, 4096, 512], P(None, 'gz', 'rows'), may hold values from -6 to 6
- block_offset: int32 [1, 8, 32, 4], P(None, 'gz', 'rows'), may hold values from -3 to 3
- row_base: int32 [1, 8, 32, 4], P(None, 'gz', 'rows'), may hold values from 0 to 127
- col_base: int32 [1, 8, 32, 4], P(None, 'gz', 'rows'), may hold values from -128 to 127
- fractions: int32 [2, 1, 8, 32, 4], P(None, None, 'gz', 'rows'), may hold values from 0 to 255
- blend: float32 [1, 8], P(None, 'gz'), may hold values from 0.72 to 0.95
- conv_first: bfloat16 [9, 32, 2], replicated, may hold values from -1.5 to 1.5
- bias_first: float32 [32], replicated, may hold values from -3 to 3
- conv_down: bfloat16 [9, 32, 32], replicated, may hold values from -0.375 to 0.375
- bias_down: float32 [32], replicated, may hold values from -3 to 3
- conv_deep: bfloat16 [2, 9, 32, 32], replicated, may hold values from -0.375 to 0.375
- bias_deep: float32 [2, 32], replicated, may hold values from -3 to 3
Outputs:
- features: bfloat16 [1, 8, 32, 2048, 256], P(None, 'gz', None, 'rows')
All inputs are finite; a program needn't handle non-finite values.
Results may differ from a plain program's by a relative error of at most 0.001.
The roundings to bfloat16 on the way count: a program that leaves them out, or rounds other values in their place, can miss the bound.
Values may be sent and summed in bfloat16 or wider, within the bound.
No kernel may reach another device: no remote copies, remote signals or barrier semaphores. Data moves between devices by JAX's collectives and lax.ppermute only.
A program may use at most 128 MiB of HBM per device.

v0:
```python
import jax
import jax.numpy as jnp
from jax import lax
from jax.experimental import pallas as pl
from jax.experimental.pallas import tpu as pltpu
from jax.sharding import PartitionSpec as P

F32 = jnp.float32
BF16 = jnp.bfloat16
VMEM = pltpu.VMEM


def vspec():
    return pl.BlockSpec(memory_space=pltpu.VMEM)


def sspec():
    return pl.BlockSpec(memory_space=pltpu.SMEM)


def aspec():
    return pl.BlockSpec(memory_space=pl.ANY)


def iota(shape, dim):
    return lax.broadcasted_iota(jnp.int32, shape, dim)


def weights_kernel(kf, kd, kp, bf, bd, bp, w1, wd, wp, bb):
    row = iota((32, 256), 0)
    lane = iota((32, 256), 1)

    def place(dr):
        return jnp.where(lane == row + 32 * dr, 1.0, 0.0).astype(BF16)

    spots = [place(dr) for dr in range(3)]

    def base(taps):
        return sum(jnp.dot(taps[dr], spots[dr], preferred_element_type=F32) for dr in range(3))

    within = lane & 31
    quarter = (lane >> 5) & 3
    for phase in range(2):
        acc = jnp.zeros((32, 256), F32)
        for dr in range(3):
            for dx in range(3):
                tap = kf[3 * dr + dx].astype(F32)
                value = jnp.where(lane < 128, tap[:, 0:1], tap[:, 1:2])
                hit = (quarter == dx + phase) & (within == 10 + dr)
                acc = acc + jnp.where(hit, value, 0.0)
        for r in range(16):
            moved = acc if r == 0 else pltpu.roll(acc, r, 1)
            w1[pl.ds(phase * 512 + r * 32, 32), :] = moved.astype(BF16)
    for place_at, dx in enumerate((1, 0, 2)):
        acc = base([kd[3 * dr + dx] for dr in range(3)])
        for r in range(3):
            moved = acc if r == 0 else pltpu.roll(acc, 64 * r, 1)
            wd[pl.ds(place_at * 96 + r * 32, 32), :] = moved.astype(BF16)
    for layer in range(2):
        for dx in range(3):
            acc = base([kp[layer, 3 * dr + dx] for dr in range(3)])
            for r in range(6):
                moved = acc if r == 0 else pltpu.roll(acc, 32 * r, 1)
                wp[layer, pl.ds(dx * 192 + r * 32, 32), :] = moved.astype(BF16)
    diagonal = iota((32, 32), 0) == iota((32, 32), 1)
    for k, line in enumerate((bf[...], bd[...], bp[0:1, :], bp[1:2, :])):
        column = jnp.sum(jnp.where(diagonal, line, 0.0), axis=1, keepdims=True)
        bb[k] = jnp.broadcast_to(column, (32, 256))


def make_weights(conv_first, conv_down, conv_deep, bias_first, bias_down, bias_deep):
    return pl.pallas_call(
        weights_kernel,
        out_shape=(
            jax.ShapeDtypeStruct((1024, 256), BF16),
            jax.ShapeDtypeStruct((288, 256), BF16),
            jax.ShapeDtypeStruct((2, 576, 256), BF16),
            jax.ShapeDtypeStruct((4, 32, 256), F32),
        ),
        in_specs=[vspec()] * 6,
        out_specs=(vspec(),) * 4,
        cost_estimate=pl.CostEstimate(flops=20_000_000, bytes_accessed=2_000_000, transcendentals=0),
        name="weights",
    )(conv_first, conv_down, conv_deep, bias_first[None], bias_down[None], bias_deep)


OFFSETS = (0, 1, 2, -1, -2, 3, 4, -3, -4)


def warp_kernel(offs, base, cols, frac, blend, *refs):
    blocks, (pay, enc, S, MJ, MV, sems) = refs[:9], refs[9:]
    core = lax.rem(lax.axis_index("rows"), 2)
    sign = 1 - 2 * core
    copies = []
    for k, off in enumerate(OFFSETS):
        copies.append(pltpu.make_async_copy(blocks[k], S.at[4 + sign * off], sems.at[k]))
    for copy in copies:
        copy.start()
    mats = []
    for j in range(4):
        lo, hi = max(j - 1, 0), min(j + 1, 3)
        wide = (hi - lo + 1) * 128
        src = iota((wide, 128), 0) + (lo - j) * 128
        n = iota((wide, 128), 1)
        if j % 2 == 0:
            x = jnp.where(n < 64, 2 * n, 2 * n - 127)
        else:
            x = jnp.where(n < 64, 2 * n + 1, 2 * n - 128)
        q = frac[1, 0, 0, 0, j].astype(F32) * (1.0 / 256.0)
        target = cols[0, 0, 0, j] + x
        mat = jnp.where(src == target, 1.0 - q, 0.0) + jnp.where(src == target + 1, q, 0.0)
        mats.append(mat.astype(BF16))
    for copy in copies:
        copy.wait()
    for j in range(4):
        lo, hi = max(j - 1, 0), min(j + 1, 3)
        o = offs[0, 0, 0, j]
        for half in range(2):
            window = S[o + 4 + half, :, lo * 128 : (hi + 1) * 128]
            out = jnp.dot(window, mats[j], preferred_element_type=F32)
            MJ[j, half * 128 : (half + 1) * 128, :] = out.astype(BF16).astype(F32)
    lane1 = iota((136, 128), 1)
    for pair in range(2):
        a = MJ[2 * pair, pl.ds(base[0, 0, 0, 2 * pair], 136), :]
        b = MJ[2 * pair + 1, pl.ds(base[0, 0, 0, 2 * pair + 1], 136), :]
        MV[:, pair * 128 : (pair + 1) * 128] = jnp.where(lane1 < 64, a, b)
        MV[:, 256 + pair * 128 : 256 + (pair + 1) * 128] = pltpu.roll(
            jnp.where(lane1 < 64, b, a), 64, 1
        )
    lane = iota((8, 512), 1)
    row = iota((8, 512), 0)
    which = (lane >> 6) & 3
    p = jnp.zeros((8, 512), F32)
    for j in range(4):
        p = jnp.where(which == j, frac[0, 0, 0, 0, j].astype(F32) * (1.0 / 256.0), p)
    rate = jnp.full((8, 512), blend[0, 0], F32)
    top = rate.astype(BF16).astype(F32)
    mid = (rate - top).astype(BF16).astype(F32)
    low = rate - top - mid
    extra = jnp.where(row == 1, p, jnp.where(row == 2, top, jnp.where(row == 3, mid, low)))
    extra = jnp.where(row > 4, 0.0, extra)
    p16 = jnp.concatenate([p, p], axis=0)
    for k in range(8):
        here = MV[16 * k : 16 * k + 16, :]
        below = MV[16 * k + 1 : 16 * k + 17, :]
        enc[16 * k : 16 * k + 16, :] = ((1.0 - p16) * here + p16 * below).astype(BF16)
        pay[k, 0:16, :] = here.astype(BF16)
        tail = MV[16 * k + 16 : 16 * k + 24, :]
        pay[k, 16:24, :] = jnp.where(row == 0, tail, extra).astype(BF16)


def make_warp(offs, base, cols, frac, blend, blocks):
    return pl.pallas_call(
        warp_kernel,
        out_shape=(
            jax.ShapeDtypeStruct((8, 24, 512), BF16),
            jax.ShapeDtypeStruct((128, 512), BF16),
        ),
        in_specs=[sspec()] * 5 + [aspec()] * 9,
        out_specs=(vspec(), vspec()),
        scratch_shapes=[
            VMEM((9, 128, 512), BF16),
            VMEM((4, 264, 128), F32),
            VMEM((136, 512), F32),
            pltpu.SemaphoreType.DMA((9,)),
        ],
        name="warp",
    )(offs, base, cols, frac, blend, *blocks)


def prior_kernel(got, out, M):
    state = jnp.zeros((16, 512), F32)
    for s in range(8):
        out[s] = state.astype(BF16)
        if s == 7:
            break
        M[s] = got[s].astype(F32)
        p = M[s, 17:18, :]
        rate = M[s, 18:19, :] + M[s, 19:20, :] + M[s, 20:21, :]
        warped = (1.0 - p) * M[s, 0:16, :] + p * M[s, 1:17, :]
        state = rate * state + (1.0 - rate) * warped


def make_prior(got):
    return pl.pallas_call(
        prior_kernel,
        out_shape=jax.ShapeDtypeStruct((8, 16, 512), BF16),
        in_specs=[vspec()],
        out_specs=vspec(),
        scratch_shapes=[VMEM((7, 24, 512), F32)],
        name="prior",
    )(got)


def encoder_kernel(enc, prior, inner, outer, w1, wd, wp, bb, out, AF, HE, HO, D, T, FS):
    place = lax.axis_index("rows")
    core = lax.rem(place, 2)
    is_top = core == 0
    lane = iota((16, 256), 1)
    zeros8 = jnp.zeros((8, 512), F32)

    def fill(ch, tile, value):
        even, odd = value[:, :256], value[:, 256:]
        rows = pl.ds(16 * tile, 16)
        AF[4 * ch, rows, :] = jnp.where(lane == 0, 0.0, pltpu.roll(odd, 1, 1)).astype(BF16)
        AF[4 * ch + 1, rows, :] = even.astype(BF16)
        AF[4 * ch + 2, rows, :] = odd.astype(BF16)
        AF[4 * ch + 3, rows, :] = jnp.where(lane == 255, 0.0, pltpu.roll(even, 255, 1)).astype(BF16)

    for ch in range(2):
        a = inner[ch].astype(F32)
        b = outer[ch].astype(F32)
        above = jnp.where(is_top, b[8:16], a[8:16])
        below = jnp.where(is_top, a[0:8], b[0:8])
        fill(ch, 0, jnp.concatenate([zeros8, above], axis=0))
        fill(ch, 9, jnp.concatenate([below, zeros8], axis=0))
    for k in range(8):
        fill(0, k + 1, enc[16 * k : 16 * k + 16, :].astype(F32))
        fill(1, k + 1, prior[k].astype(F32))

    def spread(k, n):
        return jnp.concatenate([bb[k]] * n, axis=0)

    bias16 = spread(0, 16)
    for g in range(9):
        data = AF[:, 16 * g : 16 * g + 32, :].reshape(256, 256)
        for phase, H in enumerate((HE, HO)):
            got = jnp.dot(w1[512 * phase : 512 * phase + 512, :], data, preferred_element_type=F32)
            H[512 * g : 512 * g + 512, :] = jnp.maximum(got + bias16, 0.0).astype(BF16)

    @pl.when(place == 0)
    def _():
        HE[0:160, :] = jnp.zeros((160, 256), BF16)
        HO[0:160, :] = jnp.zeros((160, 256), BF16)

    @pl.when(place == 31)
    def _():
        HE[4256:4608, :] = jnp.zeros((352, 256), BF16)
        HO[4256:4608, :] = jnp.zeros((352, 256), BF16)

    def right(v):
        at = iota(v.shape, 1)
        return jnp.where(at == 0, 0.0, pltpu.roll(v, 1, 1))

    def left(v):
        at = iota(v.shape, 1)
        return jnp.where(at == 255, 0.0, pltpu.roll(v, 255, 1))

    bias3 = spread(1, 3)
    for g in range(23):
        even = jnp.dot(wd[0:96, :], HE[192 * g : 192 * g + 256, :], preferred_element_type=F32)
        odd = jnp.dot(wd[96:288, :], HO[192 * g : 192 * g + 256, :], preferred_element_type=F32)
        total = even + right(odd[0:96]) + odd[96:192] + bias3
        D[96 * g : 96 * g + 96, :] = jnp.maximum(total, 0.0).astype(BF16)

    @pl.when(place == 0)
    def _():
        D[0:64, :] = jnp.zeros((64, 256), BF16)

    @pl.when(place == 31)
    def _():
        D[2112:2208, :] = jnp.zeros((96, 256), BF16)

    bias6 = spread(2, 6)
    for g in range(11):
        got = jnp.dot(wp[0], D[192 * g : 192 * g + 256, :], preferred_element_type=F32)
        total = got[192:384] + right(got[0:192]) + left(got[384:576]) + bias6
        T[192 * g : 192 * g + 192, :] = jnp.maximum(total, 0.0).astype(BF16)
    T[2112:2176, :] = jnp.zeros((64, 256), BF16)

    @pl.when(place == 0)
    def _():
        T[0:32, :] = jnp.zeros((32, 256), BF16)

    @pl.when(place == 31)
    def _():
        T[2080:2112, :] = jnp.zeros((32, 256), BF16)

    bias7 = spread(3, 6)
    for g in range(11):
        got = jnp.dot(wp[1], T[192 * g : 192 * g + 256, :], preferred_element_type=F32)
        total = got[192:384] + right(got[0:192]) + left(got[384:576]) + bias7
        for half in range(2):
            FS[half, 192 * g : 192 * g + 192, :] = total[:, 128 * half : 128 * half + 128]
    for ch in range(32):
        for half in range(2):
            out[0, 0, ch, :, 128 * half : 128 * half + 128] = FS[
                half, pl.ds(ch, 64, stride=32), :
            ].astype(BF16)


def make_encoder(enc, prior, inner, outer, w1, wd, wp, bb):
    return pl.pallas_call(
        encoder_kernel,
        out_shape=jax.ShapeDtypeStruct((1, 1, 32, 64, 256), BF16),
        in_specs=[vspec()] * 8,
        out_specs=vspec(),
        scratch_shapes=[
            VMEM((8, 160, 256), BF16),
            VMEM((4608, 256), BF16),
            VMEM((4608, 256), BF16),
            VMEM((2208, 256), BF16),
            VMEM((2176, 256), BF16),
            VMEM((2, 2112, 128), F32),
        ],
        name="encoder",
    )(enc, prior, inner, outer, w1, wd, wp, bb)


def pairs(target):
    return [(i, target(i)) for i in range(32) if 0 <= target(i) < 32]


SWAP = pairs(lambda i: i ^ 1)
OUTWARD = pairs(lambda i: i - 2 if i % 2 == 0 else i + 2)
INWARD = pairs(lambda i: i + 2 if i % 2 == 0 else i - 2)
LAST = [(i, t) for i, t in INWARD if i % 2 == 1]
ACROSS = pairs(lambda i: i - 1 if i % 2 == 0 else i + 1)


def per_device(
    sections, block_offset, row_base, col_base, fractions, blend,
    conv_first, bias_first, conv_down, bias_down, conv_deep, bias_deep,
):
    def send(value, route):
        return lax.ppermute(value, "rows", route)

    own = sections[0, 0]
    p1 = send(own, OUTWARD)
    p2 = send(own, INWARD)
    a = send(own, SWAP)
    f1 = send(p1, OUTWARD)
    f2 = send(p2, LAST)
    sp1 = send(p1, SWAP)
    sp2 = send(p2, SWAP)
    sf1 = send(f1, SWAP)
    w1, wd, wp, bb = make_weights(
        conv_first, conv_down, conv_deep, bias_first, bias_down, bias_deep
    )
    pay, enc = make_warp(
        block_offset, row_base, col_base, fractions, blend,
        (own, a, p1, sp1, p2, sp2, f1, sf1, f2),
    )
    got = lax.all_to_all(pay, "gz", 0, 0)
    prior = lax.all_to_all(make_prior(got), "gz", 0, 0)
    edges = jnp.stack(
        [
            jnp.concatenate([enc[0:8], enc[120:128]], axis=0),
            jnp.concatenate([prior[0, 0:8], prior[7, 8:16]], axis=0),
        ]
    )
    inner = send(edges, SWAP)
    outer = send(edges, ACROSS)
    return make_encoder(enc, prior, inner, outer, w1, wd, wp, bb)


def solution(mesh):
    return jax.shard_map(
        per_device,
        mesh=mesh,
        in_specs=(
            P(None, "gz", "rows", None),
            P(None, "gz", "rows", None),
            P(None, "gz", "rows", None),
            P(None, "gz", "rows", None),
            P(None, None, "gz", "rows", None),
            P(None, "gz"),
            P(), P(), P(), P(), P(), P(),
        ),
        out_specs=P(None, "gz", None, "rows", None),
        check_vma=False,
    )
```

profile of v0, /device:TPU:7, one launch (start us, length us, event | category | flops | bytes accessed | tf_op | source)
XLA Modules:
  0.0 76.3 jit_solution(9515240029859946761)
XLA Ops:
  0.0 3.2 %collective-permute-start.1 = (bf16[128,512]{1,0:T(8,128)(2,1)}, bf16[128,512]{1,0:T(8,128)(2,1)S(1)}, u32[]{:S(2)}, u32[]{:S(2)}) collective-permute-start(bf16[128,512]{1,0:T(8,128)(2,1)} %bitcast.11), channel_id=1, source_target_pairs={{1,3},{2,0},{3,5},{4,2},{5,7},{6,4},{7,9},{8,6},{9,11},{10,8},{11,... | collective-permute-start | bytes 393224 | tf_op jit(solution)/shard_map/ppermute | solution.py:326
  3.2 4.2 %collective-permute-start.3 = (bf16[128,512]{1,0:T(8,128)(2,1)}, bf16[128,512]{1,0:T(8,128)(2,1)S(1)}, u32[]{:S(2)}, u32[]{:S(2)}) collective-permute-start(bf16[128,512]{1,0:T(8,128)(2,1)} %bitcast.12), channel_id=1, source_target_pairs={{0,2},{2,4},{3,1},{4,6},{5,3},{6,8},{7,5},{8,10},{9,7},{10,12},{11... | collective-permute-start | bytes 393224 | tf_op jit(solution)/shard_map/ppermute | solution.py:326
  7.4 0.6 collective-permute-done.1.refs_2_
  8.0 1.9 %collective-permute-start.5 = (bf16[128,512]{1,0:T(8,128)(2,1)S(1)}, bf16[128,512]{1,0:T(8,128)(2,1)S(1)}, u32[]{:S(2)}, u32[]{:S(2)}) collective-permute-start(bf16[128,512]{1,0:T(8,128)(2,1)S(1)} %collective-permute-done.1.refs_2_), channel_id=1, source_target_pairs={{1,3},{2,0},{3,5},{4,2},{5,7},{6,4},{7,9},{8,6},{9,11},{10,8},{11,... | collective-permute-start | bytes 393224 | tf_op jit(solution)/shard_map/ppermute | solution.py:326
  9.9 5.2 %collective-permute-start = (bf16[128,512]{1,0:T(8,128)(2,1)}, bf16[128,512]{1,0:T(8,128)(2,1)S(1)}, u32[]{:S(2)}, u32[]{:S(2)}) collective-permute-start(bf16[128,512]{1,0:T(8,128)(2,1)} %bitcast.13), channel_id=1, source_target_pairs={{0,1},{1,0},{2,3},{3,2},{4,5},{5,4},{6,7},{7,6},{8,9},{9,8},{10,11... | collective-permute-start | bytes 393224 | tf_op jit(solution)/shard_map/ppermute | solution.py:326
  15.2 0.0 collective-permute-done.3.refs_4_
  15.2 1.9 %collective-permute-start.7 = (bf16[128,512]{1,0:T(8,128)(2,1)S(1)}, bf16[128,512]{1,0:T(8,128)(2,1)S(1)}, u32[]{:S(2)}, u32[]{:S(2)}) collective-permute-start(bf16[128,512]{1,0:T(8,128)(2,1)S(1)} %collective-permute-done.3.refs_4_), channel_id=1, source_target_pairs={{3,1},{5,3},{7,5},{9,7},{11,9},{13,11},{15,13},{17,15},{19,17},{21... | collective-permute-start | bytes 393224 | tf_op jit(solution)/shard_map/ppermute | solution.py:326
  17.1 0.1 collective-permute-start.4
  17.2 0.5 collective-permute-start.2
  17.7 0.0 collective-permute-done.5.refs_6_
  17.7 0.1 collective-permute-start.6
  18.4 0.0 collective-permute-done.refs_1_
  18.5 2.4 %collective-permute-done.7.refs_8_ = bf16[128,512]{1,0:T(8,128)(2,1)S(1)} collective-permute-done((bf16[128,512]{1,0:T(8,128)(2,1)S(1)}, bf16[128,512]{1,0:T(8,128)(2,1)S(1)}, u32[]{:S(2)}, u32[]{:S(2)}) %collective-permute-start.7) | collective-permute-done | bytes 131104 | tf_op jit(solution)/shard_map/ppermute | solution.py:326
  20.9 0.0 collective-permute-done.4.refs_5_
  20.9 0.6 copy-done.5
  21.5 0.1 copy-done.6
  21.6 0.0 copy-done.7
  21.6 0.6 copy-done.8
  22.3 3.3 %warp.1 = (bf16[8,24,512]{2,1,0:T(8,128)(2,1)}, bf16[128,512]{1,0:T(8,128)(2,1)}) custom-call(s32[1,1,1,4]{3,2,1,0:T(1,128)} %offs.1, s32[1,1,1,4]{3,2,1,0:T(1,128)} %base.1, s32[1,1,1,4]{3,2,1,0:T(1,128)} %cols.1, s32[2,1,1,1,4]{4,3,2,1,0:T(1,128)} %frac.1, f32[1,1]{1,0:T(1,128)S(6)} %copy.14.blend, bf16[128,512]{1,0:T(8,128)(2,1)} %bitcast.14, ...), custom_call_target="tpu_custom_call" | custom-call | tf_op jit(solution)/shard_map/warp/pallas_call | solution.py:153
  25.6 17.9 %all_to_all.10.got = bf16[8,24,512]{2,1,0:T(8,128)(2,1)} all-to-all(bf16[8,24,512]{2,1,0:T(8,128)(2,1)} %get-tuple-element.12), channel_id=1, replica_groups=mesh['gz'=8,'rows'=32] {'gz'}, dimensions={0} | all-to-all | bytes 393216 | tf_op jit(solution)/shard_map/all_to_all | solution.py:344
  43.4 1.7 %prior.1 = bf16[8,16,512]{2,1,0:T(8,128)(2,1)} custom-call(bf16[8,24,512]{2,1,0:T(8,128)(2,1)} %all_to_all.10.got), custom_call_target="tpu_custom_call" | custom-call | tf_op jit(solution)/shard_map/prior/pallas_call | solution.py:185
  45.1 3.4 %all-to-all-start.1 = ((bf16[8,16,512]{2,1,0:T(8,128)(2,1)}), bf16[8,16,512]{2,1,0:T(8,128)(2,1)S(1)}, u32[]{:S(2)}, u32[]{:S(2)}) async-start(bf16[8,16,512]{2,1,0:T(8,128)(2,1)} %prior.1), calls=%async_computation.1 | async-start | bytes 262144 | tf_op jit(solution)/shard_map/all_to_all | solution.py:345
  48.5 0.7 fusion
  49.2 8.2 %all-to-all-done.1.prior = bf16[8,16,512]{2,1,0:T(8,128)(2,1)S(1)} async-done(((bf16[8,16,512]{2,1,0:T(8,128)(2,1)}), bf16[8,16,512]{2,1,0:T(8,128)(2,1)S(1)}, u32[]{:S(2)}, u32[]{:S(2)}) %all-to-all-start.1) | async-done | bytes 131104 | tf_op jit(solution)/shard_map/all_to_all | solution.py:345
  57.5 0.0 copy-start.11
  57.5 3.8 %collective-permute-start.9 = (bf16[2,16,512]{2,1,0:T(8,128)(2,1)S(1)}, bf16[2,16,512]{2,1,0:T(8,128)(2,1)S(1)}, u32[]{:S(2)}, u32[]{:S(2)}) collective-permute-start(bf16[2,16,512]{2,1,0:T(8,128)(2,1)S(1)} %pad_maximum_fusion), channel_id=1, source_target_pairs={{1,2},{2,1},{3,4},{4,3},{5,6},{6,5},{7,8},{8,7},{9,10},{10,9},{11,... | collective-permute-start | bytes 98312 | tf_op jit(solution)/shard_map/ppermute | solution.py:326
  61.3 1.4 %collective-permute-start.8 = (bf16[2,16,512]{2,1,0:T(8,128)(2,1)S(1)}, bf16[2,16,512]{2,1,0:T(8,128)(2,1)S(1)}, u32[]{:S(2)}, u32[]{:S(2)}) collective-permute-start(bf16[2,16,512]{2,1,0:T(8,128)(2,1)S(1)} %pad_maximum_fusion), channel_id=1, source_target_pairs={{0,1},{1,0},{2,3},{3,2},{4,5},{5,4},{6,7},{7,6},{8,9},{9,8},{10,11... | collective-permute-start | bytes 98312 | tf_op jit(solution)/shard_map/ppermute | solution.py:326
  62.7 0.8 %copy.13.kf = bf16[9,32,2]{2,1,0:T(8,128)(2,1)} copy(bf16[9,32,2]{1,2,0:T(2,128)(2,1)S(1)} %copy-done.11) | data formatting | bytes 2304 | tf_op args[6]
  63.5 2.6 %weights.1 = (bf16[1024,256]{1,0:T(8,128)(2,1)}, bf16[288,256]{1,0:T(8,128)(2,1)}, bf16[2,576,256]{2,1,0:T(8,128)(2,1)}, f32[4,32,256]{2,1,0:T(8,128)}) custom-call(bf16[9,32,2]{2,1,0:T(8,128)(2,1)} %copy.13.kf, bf16[9,32,32]{2,1,0:T(8,128)(2,1)} %kd.1, bf16[2,9,32,32]{3,2,1,0:T(8,128)(2,1)} %kp.1, f32[1,32]{1,0:T(1,128)} %bitcast.15, f32[1,32]{1,0:T(1,128)} %bitcast.16, ...), custom_call_target="tpu_custom_call" | custom-call | flops 20000000 | bytes 2000000 | tf_op jit(solution)/shard_map/weights/pallas_call | solution.py:72
  66.1 0.6 copy-done.9
  66.7 0.0 copy-done.10
  66.7 9.6 %encoder.1 = bf16[1,1,32,64,256]{4,3,2,1,0:T(8,128)(2,1)} custom-call(bf16[128,512]{1,0:T(8,128)(2,1)} %get-tuple-element.11.enc, bf16[8,16,512]{2,1,0:T(8,128)(2,1)} %copy-done, bf16[2,16,512]{2,1,0:T(8,128)(2,1)} %copy-done.10, bf16[2,16,512]{2,1,0:T(8,128)(2,1)} %copy-done.9, bf16[1024,256]{1,0:T(8,128)(2,1)} %get-tuple-element.13.w1, ...), custom_call_target="tpu_custom_call" | custom-call | tf_op jit(solution)/shard_map/encoder/pallas_call | solution.py:293
  (24 shorter events, 0.1 us)
Async XLA Ops:
  0.0 8.0 %collective-permute-start.1 = (bf16[128,512]{1,0:T(8,128)(2,1)}, bf16[128,512]{1,0:T(8,128)(2,1)S(1)}, u32[]{:S(2)}, u32[]{:S(2)}) collective-permute-start(bf16[128,512]{1,0:T(8,128)(2,1)} %bitcast.11), channel_id=1, source_target_pairs={{1,3},{2,0},{3,5},{4,2},{5,7},{6,4},{7,9},{8,6},{9,11},{10,8},{11,... | collective-permute-start | bytes 393224 | tf_op jit(solution)/shard_map/ppermute | solution.py:326
  3.2 12.0 %collective-permute-start.3 = (bf16[128,512]{1,0:T(8,128)(2,1)}, bf16[128,512]{1,0:T(8,128)(2,1)S(1)}, u32[]{:S(2)}, u32[]{:S(2)}) collective-permute-start(bf16[128,512]{1,0:T(8,128)(2,1)} %bitcast.12), channel_id=1, source_target_pairs={{0,2},{2,4},{3,1},{4,6},{5,3},{6,8},{7,5},{8,10},{9,7},{10,12},{11... | collective-permute-start | bytes 393224 | tf_op jit(solution)/shard_map/ppermute | solution.py:326
  8.0 12.9 %copy-start.1 = (bf16[128,512]{1,0:T(8,128)(2,1)}, bf16[128,512]{1,0:T(8,128)(2,1)S(1)}, u32[]{:S(2)}) copy-start(bf16[128,512]{1,0:T(8,128)(2,1)S(1)} %collective-permute-done.1.refs_2_) | copy-start | bytes 393220
  8.0 9.7 %collective-permute-start.5 = (bf16[128,512]{1,0:T(8,128)(2,1)S(1)}, bf16[128,512]{1,0:T(8,128)(2,1)S(1)}, u32[]{:S(2)}, u32[]{:S(2)}) collective-permute-start(bf16[128,512]{1,0:T(8,128)(2,1)S(1)} %collective-permute-done.1.refs_2_), channel_id=1, source_target_pairs={{1,3},{2,0},{3,5},{4,2},{5,7},{6,4},{7,9},{8,6},{9,11},{10,8},{11,... | collective-permute-start | bytes 393224 | tf_op jit(solution)/shard_map/ppermute | solution.py:326
  9.9 8.5 %collective-permute-start = (bf16[128,512]{1,0:T(8,128)(2,1)}, bf16[128,512]{1,0:T(8,128)(2,1)S(1)}, u32[]{:S(2)}, u32[]{:S(2)}) collective-permute-start(bf16[128,512]{1,0:T(8,128)(2,1)} %bitcast.13), channel_id=1, source_target_pairs={{0,1},{1,0},{2,3},{3,2},{4,5},{5,4},{6,7},{7,6},{8,9},{9,8},{10,11... | collective-permute-start | bytes 393224 | tf_op jit(solution)/shard_map/ppermute | solution.py:326
  15.2 5.8 %copy-start.2 = (bf16[128,512]{1,0:T(8,128)(2,1)}, bf16[128,512]{1,0:T(8,128)(2,1)S(1)}, u32[]{:S(2)}) copy-start(bf16[128,512]{1,0:T(8,128)(2,1)S(1)} %collective-permute-done.3.refs_4_) | copy-start | bytes 393220
  15.2 5.7 %collective-permute-start.7 = (bf16[128,512]{1,0:T(8,128)(2,1)S(1)}, bf16[128,512]{1,0:T(8,128)(2,1)S(1)}, u32[]{:S(2)}, u32[]{:S(2)}) collective-permute-start(bf16[128,512]{1,0:T(8,128)(2,1)S(1)} %collective-permute-done.3.refs_4_), channel_id=1, source_target_pairs={{3,1},{5,3},{7,5},{9,7},{11,9},{13,11},{15,13},{17,15},{19,17},{21... | collective-permute-start | bytes 393224 | tf_op jit(solution)/shard_map/ppermute | solution.py:326
  17.1 3.8 %collective-permute-start.4 = (bf16[128,512]{1,0:T(8,128)(2,1)S(1)}, bf16[128,512]{1,0:T(8,128)(2,1)S(1)}, u32[]{:S(2)}, u32[]{:S(2)}) collective-permute-start(bf16[128,512]{1,0:T(8,128)(2,1)S(1)} %collective-permute-done.3.refs_4_), channel_id=1, source_target_pairs={{0,1},{1,0},{2,3},{3,2},{4,5},{5,4},{6,7},{7,6},{8,9},{9,8},{10,11... | collective-permute-start | bytes 393224 | tf_op jit(solution)/shard_map/ppermute | solution.py:326
  17.2 3.7 %collective-permute-start.2 = (bf16[128,512]{1,0:T(8,128)(2,1)S(1)}, bf16[128,512]{1,0:T(8,128)(2,1)S(1)}, u32[]{:S(2)}, u32[]{:S(2)}) collective-permute-start(bf16[128,512]{1,0:T(8,128)(2,1)S(1)} %collective-permute-done.1.refs_2_), channel_id=1, source_target_pairs={{0,1},{1,0},{2,3},{3,2},{4,5},{5,4},{6,7},{7,6},{8,9},{9,8},{10,11... | collective-permute-start | bytes 393224 | tf_op jit(solution)/shard_map/ppermute | solution.py:326
  17.7 3.2 %copy-start.3 = (bf16[128,512]{1,0:T(8,128)(2,1)}, bf16[128,512]{1,0:T(8,128)(2,1)S(1)}, u32[]{:S(2)}) copy-start(bf16[128,512]{1,0:T(8,128)(2,1)S(1)} %collective-permute-done.5.refs_6_) | copy-start | bytes 393220
  17.7 3.2 %collective-permute-start.6 = (bf16[128,512]{1,0:T(8,128)(2,1)S(1)}, bf16[128,512]{1,0:T(8,128)(2,1)S(1)}, u32[]{:S(2)}, u32[]{:S(2)}) collective-permute-start(bf16[128,512]{1,0:T(8,128)(2,1)S(1)} %collective-permute-done.5.refs_6_), channel_id=1, source_target_pairs={{0,1},{1,0},{2,3},{3,2},{4,5},{5,4},{6,7},{7,6},{8,9},{9,8},{10,11... | collective-permute-start | bytes 393224 | tf_op jit(solution)/shard_map/ppermute | solution.py:326
  18.5 2.5 %copy-start.4 = (bf16[128,512]{1,0:T(8,128)(2,1)}, bf16[128,512]{1,0:T(8,128)(2,1)S(1)}, u32[]{:S(2)}) copy-start(bf16[128,512]{1,0:T(8,128)(2,1)S(1)} %collective-permute-done.refs_1_) | copy-start | bytes 393220
  20.9 0.7 copy-start.5
  20.9 0.7 copy-start.6
  20.9 0.7 copy-start.7
  21.6 0.6 copy-start.8
  45.1 12.3 %all-to-all-start.1 = ((bf16[8,16,512]{2,1,0:T(8,128)(2,1)}), bf16[8,16,512]{2,1,0:T(8,128)(2,1)S(1)}, u32[]{:S(2)}, u32[]{:S(2)}) async-start(bf16[8,16,512]{2,1,0:T(8,128)(2,1)} %prior.1), calls=%async_computation.1 | async-start | bytes 262144 | tf_op jit(solution)/shard_map/all_to_all | solution.py:345
  57.4 8.6 %copy-start = (bf16[8,16,512]{2,1,0:T(8,128)(2,1)}, bf16[8,16,512]{2,1,0:T(8,128)(2,1)S(1)}, u32[]{:S(2)}) copy-start(bf16[8,16,512]{2,1,0:T(8,128)(2,1)S(1)} %all-to-all-done.1.prior) | copy-start | bytes 393220
  57.5 5.3 %copy-start.11 = (bf16[9,32,2]{1,2,0:T(2,128)(2,1)S(1)}, bf16[9,32,2]{1,2,0:T(2,128)(2,1)}, u32[]{:S(2)}) copy-start(bf16[9,32,2]{1,2,0:T(2,128)(2,1)} %param.18) | copy-start | bytes 3460
  57.5 8.6 %collective-permute-start.9 = (bf16[2,16,512]{2,1,0:T(8,128)(2,1)S(1)}, bf16[2,16,512]{2,1,0:T(8,128)(2,1)S(1)}, u32[]{:S(2)}, u32[]{:S(2)}) collective-permute-start(bf16[2,16,512]{2,1,0:T(8,128)(2,1)S(1)} %pad_maximum_fusion), channel_id=1, source_target_pairs={{1,2},{2,1},{3,4},{4,3},{5,6},{6,5},{7,8},{8,7},{9,10},{10,9},{11,... | collective-permute-start | bytes 98312 | tf_op jit(solution)/shard_map/ppermute | solution.py:326
  61.3 4.8 %collective-permute-start.8 = (bf16[2,16,512]{2,1,0:T(8,128)(2,1)S(1)}, bf16[2,16,512]{2,1,0:T(8,128)(2,1)S(1)}, u32[]{:S(2)}, u32[]{:S(2)}) collective-permute-start(bf16[2,16,512]{2,1,0:T(8,128)(2,1)S(1)} %pad_maximum_fusion), channel_id=1, source_target_pairs={{0,1},{1,0},{2,3},{3,2},{4,5},{5,4},{6,7},{7,6},{8,9},{9,8},{10,11... | collective-permute-start | bytes 98312 | tf_op jit(solution)/shard_map/ppermute | solution.py:326
  66.1 0.6 copy-start.9
  66.1 0.6 copy-start.10
where the time goes:
time: 76.9 us; the launch traced here: 76.3 us
  starting transfers between devices  25.7 us (33%)
  blocking collectives  17.9 us (23%)
  Pallas kernels  17.1 us (22%)
  waiting for transfers between devices  11.3 us (15%)
  local copies, waits for them, and re-layouts  3.44 us (4%)
  between operations  0.84 us (1%)
    ppermute x10, starting transfers between devices, send(): return lax.ppermute(value, 'rows', route)  22.3 us
    all_to_all x1, blocking collectives, per_device(): got = lax.all_to_all(pay, 'gz', 0, 0)  17.9 us
    pallas_call x1, Pallas kernels, make_encoder(): pl.pallas_call(encoder_kernel, out_shape=jax.ShapeDtypeStruct((1, 1, 32,...  9.56 us
    all_to_all x1, waiting for transfers between devices, per_device(): prior = lax.all_to_all(make_prior(got), 'gz', 0, 0)  8.23 us
    all_to_all x1, starting transfers between devices, per_device(): prior = lax.all_to_all(make_prior(got), 'gz', 0, 0)  3.37 us
    pallas_call x1, Pallas kernels, make_warp(): pl.pallas_call(warp_kernel, out_shape=(jax.ShapeDtypeStruct((8, 24, 512),...  3.28 us
    ppermute x10, waiting for transfers between devices, send(): return lax.ppermute(value, 'rows', route)  3.05 us
    unnamed x25, local copies, waits for them, and re-layouts  2.72 us
  transfers between devices with their start and end apart: 11, of which 3 were waited for; matrix products, arithmetic and copies ran while one was open for 2% of the time, Pallas kernels for 3%

commit v1 on v0

--- a/solution.py
+++ b/solution.py
@@ -37,6 +37,11 @@
 
     def base(taps):
         return sum(jnp.dot(taps[dr], spots[dr], preferred_element_type=F32) for dr in range(3))
+
+    diagonal = iota((32, 32), 0) == iota((32, 32), 1)
+
+    def upright(line):
+        return jnp.sum(jnp.where(diagonal, line, 0.0), axis=1, keepdims=True)
 
     within = lane & 31
     quarter = (lane >> 5) & 3
@@ -45,7 +50,7 @@
         for dr in range(3):
             for dx in range(3):
                 tap = kf[3 * dr + dx].astype(F32)
-                value = jnp.where(lane < 128, tap[:, 0:1], tap[:, 1:2])
+                value = jnp.where(lane < 128, upright(tap[0:1, :]), upright(tap[1:2, :]))
                 hit = (quarter == dx + phase) & (within == 10 + dr)
                 acc = acc + jnp.where(hit, value, 0.0)
         for r in range(16):
@@ -62,10 +67,8 @@
             for r in range(6):
                 moved = acc if r == 0 else pltpu.roll(acc, 32 * r, 1)
                 wp[layer, pl.ds(dx * 192 + r * 32, 32), :] = moved.astype(BF16)
-    diagonal = iota((32, 32), 0) == iota((32, 32), 1)
     for k, line in enumerate((bf[...], bd[...], bp[0:1, :], bp[1:2, :])):
-        column = jnp.sum(jnp.where(diagonal, line, 0.0), axis=1, keepdims=True)
-        bb[k] = jnp.broadcast_to(column, (32, 256))
+        bb[k] = jnp.broadcast_to(upright(line), (32, 256))
 
 
 def make_weights(conv_first, conv_down, conv_deep, bias_first, bias_down, bias_deep):
@@ -80,8 +83,9 @@
         in_specs=[vspec()] * 6,
         out_specs=(vspec(),) * 4,
         cost_estimate=pl.CostEstimate(flops=20_000_000, bytes_accessed=2_000_000, transcendentals=0),
+        compiler_params=pltpu.CompilerParams(vmem_limit_bytes=6 << 20),
         name="weights",
-    )(conv_first, conv_down, conv_deep, bias_first[None], bias_down[None], bias_deep)
+    )(conv_first.transpose(0, 2, 1), conv_down, conv_deep, bias_first[None], bias_down[None], bias_deep)
 
 
 OFFSETS = (0, 1, 2, -1, -2, 3, 4, -3, -4)
@@ -156,7 +160,7 @@
             jax.ShapeDtypeStruct((8, 24, 512), BF16),
             jax.ShapeDtypeStruct((128, 512), BF16),
         ),
-        in_specs=[sspec()] * 5 + [aspec()] * 9,
+        in_specs=[sspec()] * 5 + [pl.BlockSpec(memory_space=pltpu.HBM)] + [aspec()] * 8,
         out_specs=(vspec(), vspec()),
         scratch_shapes=[
             VMEM((9, 128, 512), BF16),
@@ -164,6 +168,7 @@
             VMEM((136, 512), F32),
             pltpu.SemaphoreType.DMA((9,)),
         ],
+        compiler_params=pltpu.CompilerParams(vmem_limit_bytes=8 << 20),
         name="warp",
     )(offs, base, cols, frac, blend, *blocks)
 
@@ -188,6 +193,7 @@
         in_specs=[vspec()],
         out_specs=vspec(),
         scratch_shapes=[VMEM((7, 24, 512), F32)],
+        compiler_params=pltpu.CompilerParams(vmem_limit_bytes=4 << 20),
         name="prior",
     )(got)
 
@@ -248,8 +254,8 @@
 
     bias3 = spread(1, 3)
     for g in range(23):
-        even = jnp.dot(wd[0:96, :], HE[192 * g : 192 * g + 256, :], preferred_element_type=F32)
-        odd = jnp.dot(wd[96:288, :], HO[192 * g : 192 * g + 256, :], preferred_element_type=F32)
+        even = jnp.dot(wd[0:96, 0:224], HE[192 * g : 192 * g + 224, :], preferred_element_type=F32)
+        odd = jnp.dot(wd[96:288, 0:224], HO[192 * g : 192 * g + 224, :], preferred_element_type=F32)
         total = even + right(odd[0:96]) + odd[96:192] + bias3
         D[96 * g : 96 * g + 96, :] = jnp.maximum(total, 0.0).astype(BF16)
 
@@ -280,12 +286,16 @@
     for g in range(11):
         got = jnp.dot(wp[1], T[192 * g : 192 * g + 256, :], preferred_element_type=F32)
         total = got[192:384] + right(got[0:192]) + left(got[384:576]) + bias7
-        for half in range(2):
-            FS[half, 192 * g : 192 * g + 192, :] = total[:, 128 * half : 128 * half + 128]
+        for r in range(6):
+            for part in range(4):
+                for half in range(2):
+                    FS[half, part, 48 * g + 8 * r : 48 * g + 8 * r + 8, :] = total[
+                        32 * r + 8 * part : 32 * r + 8 * part + 8, 128 * half : 128 * half + 128
+                    ]
     for ch in range(32):
         for half in range(2):
             out[0, 0, ch, :, 128 * half : 128 * half + 128] = FS[
-                half, pl.ds(ch, 64, stride=32), :
+                half, ch // 8, pl.ds(ch % 8, 64, stride=8), :
             ].astype(BF16)
 
 
@@ -301,8 +311,9 @@
             VMEM((4608, 256), BF16),
             VMEM((2208, 256), BF16),
             VMEM((2176, 256), BF16),
-            VMEM((2, 2112, 128), F32),
+            VMEM((2, 4, 528, 128), F32),
         ],
+        compiler_params=pltpu.CompilerParams(vmem_limit_bytes=20 << 20),
         name="encoder",
     )(enc, prior, inner, outer, w1, wd, wp, bb)
 
@@ -342,7 +353,8 @@
         (own, a, p1, sp1, p2, sp2, f1, sf1, f2),
     )
     got = lax.all_to_all(pay, "gz", 0, 0)
-    prior = lax.all_to_all(make_prior(got), "gz", 0, 0)
+    given = make_prior(got)
+    prior = lax.all_to_all(given, "gz", 0, 0)
     edges = jnp.stack(
         [
             jnp.concatenate([enc[0:8], enc[120:128]], axis=0),

time: 76.9 us -> 70.5 us (0.917)
  the two profiles are of different devices: /device:TPU:7 before, /device:TPU:6 now
where the time goes in v1:
time: 70.5 us; the launch traced here: 70.1 us
  starting transfers between devices  23.2 us (33%)
  blocking collectives  18.8 us (27%)
  waiting for transfers between devices  14.5 us (21%)
  Pallas kernels  11.1 us (16%)
  local copies, waits for them, and re-layouts  1.59 us (2%)
  between operations  0.85 us (1%)
    ppermute x10, starting transfers between devices, send(): return lax.ppermute(value, 'rows', route)  19.7 us
    all_to_all x1, blocking collectives, per_device(): got = lax.all_to_all(pay, 'gz', 0, 0)  18.8 us
    all_to_all x1, waiting for transfers between devices, per_device(): prior = lax.all_to_all(given, 'gz', 0, 0)  10.3 us
    pallas_call x1, Pallas kernels, make_encoder(): pl.pallas_call(encoder_kernel, out_shape=jax.ShapeDtypeStruct((1, 1, 32,...  6.79 us
    ppermute x10, waiting for transfers between devices, send(): return lax.ppermute(value, 'rows', route)  4.29 us
    all_to_all x1, starting transfers between devices, per_device(): prior = lax.all_to_all(given, 'gz', 0, 0)  3.5 us
    pallas_call x1, Pallas kernels, make_warp(): pl.pallas_call(warp_kernel, out_shape=(jax.ShapeDtypeStruct((8, 24, 512),...  2.85 us
    unnamed x22, local copies, waits for them, and re-layouts  1.59 us
  transfers between devices with their start and end apart: 11, of which 5 were waited for; matrix products, arithmetic and copies ran while one was open for 0% of the time, Pallas kernels for 1%

profile of v1, /device:TPU:6, one launch (start us, length us, event | category | flops | bytes accessed | tf_op | source)
XLA Modules:
  0.0 70.1 jit_solution(8591484845534340016)
XLA Ops:
  0.0 5.3 %collective-permute-start.1 = (bf16[128,512]{1,0:T(8,128)(2,1)}, bf16[128,512]{1,0:T(8,128)(2,1)S(1)}, u32[]{:S(2)}, u32[]{:S(2)}) collective-permute-start(bf16[128,512]{1,0:T(8,128)(2,1)} %bitcast.12), channel_id=1, source_target_pairs={{1,3},{2,0},{3,5},{4,2},{5,7},{6,4},{7,9},{8,6},{9,11},{10,8},{11,... | collective-permute-start | bytes 393224 | tf_op jit(solution)/shard_map/ppermute | solution.py:337
  5.3 1.9 %collective-permute-start.3 = (bf16[128,512]{1,0:T(8,128)(2,1)}, bf16[128,512]{1,0:T(8,128)(2,1)S(1)}, u32[]{:S(2)}, u32[]{:S(2)}) collective-permute-start(bf16[128,512]{1,0:T(8,128)(2,1)} %bitcast.13), channel_id=1, source_target_pairs={{0,2},{2,4},{3,1},{4,6},{5,3},{6,8},{7,5},{8,10},{9,7},{10,12},{11... | collective-permute-start | bytes 393224 | tf_op jit(solution)/shard_map/ppermute | solution.py:337
  7.3 0.9 %collective-permute-done.1.refs_2_ = bf16[128,512]{1,0:T(8,128)(2,1)S(1)} collective-permute-done((bf16[128,512]{1,0:T(8,128)(2,1)}, bf16[128,512]{1,0:T(8,128)(2,1)S(1)}, u32[]{:S(2)}, u32[]{:S(2)}) %collective-permute-start.1) | collective-permute-done | bytes 131104 | tf_op jit(solution)/shard_map/ppermute | solution.py:337
  8.2 6.4 %collective-permute-start.5 = (bf16[128,512]{1,0:T(8,128)(2,1)S(1)}, bf16[128,512]{1,0:T(8,128)(2,1)S(1)}, u32[]{:S(2)}, u32[]{:S(2)}) collective-permute-start(bf16[128,512]{1,0:T(8,128)(2,1)S(1)} %collective-permute-done.1.refs_2_), channel_id=1, source_target_pairs={{1,3},{2,0},{3,5},{4,2},{5,7},{6,4},{7,9},{8,6},{9,11},{10,8},{11,... | collective-permute-start | bytes 393224 | tf_op jit(solution)/shard_map/ppermute | solution.py:337
  14.6 0.1 collective-permute-start
  14.7 0.0 collective-permute-done.3.refs_4_
  14.7 0.7 collective-permute-start.7
  15.3 1.8 %collective-permute-start.4 = (bf16[128,512]{1,0:T(8,128)(2,1)S(1)}, bf16[128,512]{1,0:T(8,128)(2,1)S(1)}, u32[]{:S(2)}, u32[]{:S(2)}) collective-permute-start(bf16[128,512]{1,0:T(8,128)(2,1)S(1)} %collective-permute-done.3.refs_4_), channel_id=1, source_target_pairs={{0,1},{1,0},{2,3},{3,2},{4,5},{5,4},{6,7},{7,6},{8,9},{9,8},{10,11... | collective-permute-start | bytes 393224 | tf_op jit(solution)/shard_map/ppermute | solution.py:337
  17.2 0.1 collective-permute-start.2
  17.3 0.0 collective-permute-done.5.refs_6_
  17.3 0.4 collective-permute-start.6
  18.3 0.0 collective-permute-done.refs_1_
  18.3 0.0 collective-permute-done.7.refs_8_
  18.4 0.0 collective-permute-done.4.refs_5_
  18.4 0.2 collective-permute-done.2.refs_3_
  18.5 0.2 collective-permute-done.6.refs_7_
  18.7 0.9 %copy-done.1 = bf16[1,1,128,512]{3,2,1,0:T(8,128)(2,1)S(1)} copy-done((bf16[1,1,128,512]{3,2,1,0:T(8,128)(2,1)S(1)}, bf16[1,1,128,512]{3,2,1,0:T(8,128)(2,1)}, u32[]{:S(2)}) %copy-start.1) | copy-done | bytes 131096
  19.6 2.9 %warp.1 = (bf16[8,24,512]{2,1,0:T(8,128)(2,1)S(1)}, bf16[128,512]{1,0:T(8,128)(2,1)S(1)}) custom-call(s32[1,1,1,4]{3,2,1,0:T(1,128)S(1)} %copy-done.6, s32[1,1,1,4]{3,2,1,0:T(1,128)S(1)} %copy-done.7, s32[1,1,1,4]{3,2,1,0:T(1,128)S(1)} %copy-done.8, s32[2,1,1,1,4]{4,3,2,1,0:T(1,128)S(1)} %copy-done.5, f32[1,1]{1,0:T(1,128)S(6)} %copy.13.blend, ...), custom_call_target="tpu_custom_call" | custom-call | tf_op jit(solution)/shard_map/warp/pallas_call | solution.py:157
  22.5 18.8 %all_to_all.10.got = bf16[8,24,512]{2,1,0:T(8,128)(2,1)S(1)} all-to-all(bf16[8,24,512]{2,1,0:T(8,128)(2,1)S(1)} %get-tuple-element.12), channel_id=1, replica_groups=mesh['gz'=8,'rows'=32] {'gz'}, dimensions={0} | all-to-all | bytes 393216 | tf_op jit(solution)/shard_map/all_to_all | solution.py:355
  41.3 0.8 %prior.1 = bf16[8,16,512]{2,1,0:T(8,128)(2,1)} custom-call(bf16[8,24,512]{2,1,0:T(8,128)(2,1)S(1)} %all_to_all.10.got), custom_call_target="tpu_custom_call" | custom-call | tf_op jit(solution)/shard_map/prior/pallas_call | solution.py:190
  42.1 3.5 %all-to-all-start.1 = ((bf16[8,16,512]{2,1,0:T(8,128)(2,1)}), bf16[8,16,512]{2,1,0:T(8,128)(2,1)S(1)}, u32[]{:S(2)}, u32[]{:S(2)}) async-start(bf16[8,16,512]{2,1,0:T(8,128)(2,1)} %prior.1), calls=%async_computation.1 | async-start | bytes 262144 | tf_op jit(solution)/shard_map/all_to_all | solution.py:357
  45.6 0.0 copy-start
  45.6 10.3 %all-to-all-done.1.prior = bf16[8,16,512]{2,1,0:T(8,128)(2,1)S(1)} async-done(((bf16[8,16,512]{2,1,0:T(8,128)(2,1)}), bf16[8,16,512]{2,1,0:T(8,128)(2,1)S(1)}, u32[]{:S(2)}, u32[]{:S(2)}) %all-to-all-start.1) | async-done | bytes 131104 | tf_op jit(solution)/shard_map/all_to_all | solution.py:357
  55.9 0.0 copy-start.10
  55.9 0.0 copy-start.3
  55.9 2.6 %collective-permute-start.9 = (bf16[2,16,512]{2,1,0:T(8,128)(2,1)S(1)}, bf16[2,16,512]{2,1,0:T(8,128)(2,1)S(1)}, u32[]{:S(2)}, u32[]{:S(2)}) collective-permute-start(bf16[2,16,512]{2,1,0:T(8,128)(2,1)S(1)} %pad_maximum_fusion), channel_id=1, source_target_pairs={{1,2},{2,1},{3,4},{4,3},{5,6},{6,5},{7,8},{8,7},{9,10},{10,9},{11,... | collective-permute-start | bytes 98312 | tf_op jit(solution)/shard_map/ppermute | solution.py:337
  58.5 0.4 collective-permute-start.8
  58.9 0.6 copy-done.4
  59.6 0.7 weights.1
  60.2 3.0 %collective-permute-done.9.outer = bf16[2,16,512]{2,1,0:T(8,128)(2,1)S(1)} collective-permute-done((bf16[2,16,512]{2,1,0:T(8,128)(2,1)S(1)}, bf16[2,16,512]{2,1,0:T(8,128)(2,1)S(1)}, u32[]{:S(2)}, u32[]{:S(2)}) %collective-permute-start.9) | collective-permute-done | bytes 32800 | tf_op jit(solution)/shard_map/ppermute | solution.py:337
  63.3 0.0 collective-permute-done.8.inner
  63.3 6.8 %encoder.1 = bf16[1,1,32,64,256]{4,3,2,1,0:T(8,128)(2,1)} custom-call(bf16[128,512]{1,0:T(8,128)(2,1)S(1)} %get-tuple-element.11.enc, bf16[8,16,512]{2,1,0:T(8,128)(2,1)S(1)} %all-to-all-done.1.prior, bf16[2,16,512]{2,1,0:T(8,128)(2,1)S(1)} %collective-permute-done.8.inner, bf16[2,16,512]{2,1,0:T(8,128)(2,1)S(1)} %collective-permute-done.9.outer, ...), custom_call_target="tpu_custom_call" | custom-call | tf_op jit(solution)/shard_map/encoder/pallas_call | solution.py:303
  (21 shorter events, 0.1 us)
Async XLA Ops:
  0.0 18.7 %copy-start.7 = (s32[1,1,1,4]{3,2,1,0:T(1,128)S(1)}, s32[1,1,1,4]{3,2,1,0:T(1,128)}, u32[]{:S(2)}) copy-start(s32[1,1,1,4]{3,2,1,0:T(1,128)} %base.1) | copy-start | bytes 52
  0.0 18.7 %copy-start.8 = (s32[1,1,1,4]{3,2,1,0:T(1,128)S(1)}, s32[1,1,1,4]{3,2,1,0:T(1,128)}, u32[]{:S(2)}) copy-start(s32[1,1,1,4]{3,2,1,0:T(1,128)} %cols.1) | copy-start | bytes 52
  0.0 18.7 %copy-start.5 = (s32[2,1,1,1,4]{4,3,2,1,0:T(1,128)S(1)}, s32[2,1,1,1,4]{4,3,2,1,0:T(1,128)}, u32[]{:S(2)}) copy-start(s32[2,1,1,1,4]{4,3,2,1,0:T(1,128)} %frac.1) | copy-start | bytes 100
  0.0 18.7 %copy-start.6 = (s32[1,1,1,4]{3,2,1,0:T(1,128)S(1)}, s32[1,1,1,4]{3,2,1,0:T(1,128)}, u32[]{:S(2)}) copy-start(s32[1,1,1,4]{3,2,1,0:T(1,128)} %offs.1) | copy-start | bytes 52
  0.0 8.2 %collective-permute-start.1 = (bf16[128,512]{1,0:T(8,128)(2,1)}, bf16[128,512]{1,0:T(8,128)(2,1)S(1)}, u32[]{:S(2)}, u32[]{:S(2)}) collective-permute-start(bf16[128,512]{1,0:T(8,128)(2,1)} %bitcast.12), channel_id=1, source_target_pairs={{1,3},{2,0},{3,5},{4,2},{5,7},{6,4},{7,9},{8,6},{9,11},{10,8},{11,... | collective-permute-start | bytes 393224 | tf_op jit(solution)/shard_map/ppermute | solution.py:337
  5.3 9.3 %collective-permute-start.3 = (bf16[128,512]{1,0:T(8,128)(2,1)}, bf16[128,512]{1,0:T(8,128)(2,1)S(1)}, u32[]{:S(2)}, u32[]{:S(2)}) collective-permute-start(bf16[128,512]{1,0:T(8,128)(2,1)} %bitcast.13), channel_id=1, source_target_pairs={{0,2},{2,4},{3,1},{4,6},{5,3},{6,8},{7,5},{8,10},{9,7},{10,12},{11... | collective-permute-start | bytes 393224 | tf_op jit(solution)/shard_map/ppermute | solution.py:337
  8.2 9.1 %collective-permute-start.5 = (bf16[128,512]{1,0:T(8,128)(2,1)S(1)}, bf16[128,512]{1,0:T(8,128)(2,1)S(1)}, u32[]{:S(2)}, u32[]{:S(2)}) collective-permute-start(bf16[128,512]{1,0:T(8,128)(2,1)S(1)} %collective-permute-done.1.refs_2_), channel_id=1, source_target_pairs={{1,3},{2,0},{3,5},{4,2},{5,7},{6,4},{7,9},{8,6},{9,11},{10,8},{11,... | collective-permute-start | bytes 393224 | tf_op jit(solution)/shard_map/ppermute | solution.py:337
  14.6 3.8 %collective-permute-start = (bf16[128,512]{1,0:T(8,128)(2,1)}, bf16[128,512]{1,0:T(8,128)(2,1)S(1)}, u32[]{:S(2)}, u32[]{:S(2)}) collective-permute-start(bf16[128,512]{1,0:T(8,128)(2,1)} %bitcast.14), channel_id=1, source_target_pairs={{0,1},{1,0},{2,3},{3,2},{4,5},{5,4},{6,7},{7,6},{8,9},{9,8},{10,11... | collective-permute-start | bytes 393224 | tf_op jit(solution)/shard_map/ppermute | solution.py:337
  14.7 3.7 %collective-permute-start.7 = (bf16[128,512]{1,0:T(8,128)(2,1)S(1)}, bf16[128,512]{1,0:T(8,128)(2,1)S(1)}, u32[]{:S(2)}, u32[]{:S(2)}) collective-permute-start(bf16[128,512]{1,0:T(8,128)(2,1)S(1)} %collective-permute-done.3.refs_4_), channel_id=1, source_target_pairs={{3,1},{5,3},{7,5},{9,7},{11,9},{13,11},{15,13},{17,15},{19,17},{21... | collective-permute-start | bytes 393224 | tf_op jit(solution)/shard_map/ppermute | solution.py:337
  15.3 3.0 %collective-permute-start.4 = (bf16[128,512]{1,0:T(8,128)(2,1)S(1)}, bf16[128,512]{1,0:T(8,128)(2,1)S(1)}, u32[]{:S(2)}, u32[]{:S(2)}) collective-permute-start(bf16[128,512]{1,0:T(8,128)(2,1)S(1)} %collective-permute-done.3.refs_4_), channel_id=1, source_target_pairs={{0,1},{1,0},{2,3},{3,2},{4,5},{5,4},{6,7},{7,6},{8,9},{9,8},{10,11... | collective-permute-start | bytes 393224 | tf_op jit(solution)/shard_map/ppermute | solution.py:337
  17.2 1.3 %collective-permute-start.2 = (bf16[128,512]{1,0:T(8,128)(2,1)S(1)}, bf16[128,512]{1,0:T(8,128)(2,1)S(1)}, u32[]{:S(2)}, u32[]{:S(2)}) collective-permute-start(bf16[128,512]{1,0:T(8,128)(2,1)S(1)} %collective-permute-done.1.refs_2_), channel_id=1, source_target_pairs={{0,1},{1,0},{2,3},{3,2},{4,5},{5,4},{6,7},{7,6},{8,9},{9,8},{10,11... | collective-permute-start | bytes 393224 | tf_op jit(solution)/shard_map/ppermute | solution.py:337
  17.3 1.4 %collective-permute-start.6 = (bf16[128,512]{1,0:T(8,128)(2,1)S(1)}, bf16[128,512]{1,0:T(8,128)(2,1)S(1)}, u32[]{:S(2)}, u32[]{:S(2)}) collective-permute-start(bf16[128,512]{1,0:T(8,128)(2,1)S(1)} %collective-permute-done.5.refs_6_), channel_id=1, source_target_pairs={{0,1},{1,0},{2,3},{3,2},{4,5},{5,4},{6,7},{7,6},{8,9},{9,8},{10,11... | collective-permute-start | bytes 393224 | tf_op jit(solution)/shard_map/ppermute | solution.py:337
  18.7 0.9 %copy-start.1 = (bf16[1,1,128,512]{3,2,1,0:T(8,128)(2,1)S(1)}, bf16[1,1,128,512]{3,2,1,0:T(8,128)(2,1)}, u32[]{:S(2)}) copy-start(bf16[1,1,128,512]{3,2,1,0:T(8,128)(2,1)} %param.12) | copy-start | bytes 393220
  42.1 16.8 %copy-start.2 = (bf16[9,32,32]{2,1,0:T(8,128)(2,1)S(1)}, bf16[9,32,32]{2,1,0:T(8,128)(2,1)}, u32[]{:S(2)}) copy-start(bf16[9,32,32]{2,1,0:T(8,128)(2,1)} %kd.1) | copy-start | bytes 55300
  42.1 13.8 %all-to-all-start.1 = ((bf16[8,16,512]{2,1,0:T(8,128)(2,1)}), bf16[8,16,512]{2,1,0:T(8,128)(2,1)S(1)}, u32[]{:S(2)}, u32[]{:S(2)}) async-start(bf16[8,16,512]{2,1,0:T(8,128)(2,1)} %prior.1), calls=%async_computation.1 | async-start | bytes 262144 | tf_op jit(solution)/shard_map/all_to_all | solution.py:357
  45.6 13.3 %copy-start = (bf16[2,9,32,32]{3,2,1,0:T(8,128)(2,1)S(1)}, bf16[2,9,32,32]{3,2,1,0:T(8,128)(2,1)}, u32[]{:S(2)}) copy-start(bf16[2,9,32,32]{3,2,1,0:T(8,128)(2,1)} %kp.1) | copy-start | bytes 110596
  55.9 3.0 %copy-start.9 = (f32[32]{0:T(128)S(1)}, f32[32]{0:T(128)}, u32[]{:S(2)}) copy-start(f32[32]{0:T(128)} %param.19) | copy-start | bytes 388
  55.9 3.0 %copy-start.10 = (f32[32]{0:T(128)S(1)}, f32[32]{0:T(128)}, u32[]{:S(2)}) copy-start(f32[32]{0:T(128)} %param.21) | copy-start | bytes 388
  55.9 3.0 %copy-start.3 = (bf16[9,32,2]{1,2,0:T(2,128)(2,1)S(1)}, bf16[9,32,2]{1,2,0:T(2,128)(2,1)}, u32[]{:S(2)}) copy-start(bf16[9,32,2]{1,2,0:T(2,128)(2,1)} %param.18) | copy-start | bytes 3460
  55.9 7.3 %collective-permute-start.9 = (bf16[2,16,512]{2,1,0:T(8,128)(2,1)S(1)}, bf16[2,16,512]{2,1,0:T(8,128)(2,1)S(1)}, u32[]{:S(2)}, u32[]{:S(2)}) collective-permute-start(bf16[2,16,512]{2,1,0:T(8,128)(2,1)S(1)} %pad_maximum_fusion), channel_id=1, source_target_pairs={{1,2},{2,1},{3,4},{4,3},{5,6},{6,5},{7,8},{8,7},{9,10},{10,9},{11,... | collective-permute-start | bytes 98312 | tf_op jit(solution)/shard_map/ppermute | solution.py:337
  58.5 4.8 %collective-permute-start.8 = (bf16[2,16,512]{2,1,0:T(8,128)(2,1)S(1)}, bf16[2,16,512]{2,1,0:T(8,128)(2,1)S(1)}, u32[]{:S(2)}, u32[]{:S(2)}) collective-permute-start(bf16[2,16,512]{2,1,0:T(8,128)(2,1)S(1)} %pad_maximum_fusion), channel_id=1, source_target_pairs={{0,1},{1,0},{2,3},{3,2},{4,5},{5,4},{6,7},{7,6},{8,9},{9,8},{10,11... | collective-permute-start | bytes 98312 | tf_op jit(solution)/shard_map/ppermute | solution.py:337
  58.9 0.7 copy-start.4

commit v2 on v1

--- a/solution.py
+++ b/solution.py
@@ -16,10 +16,6 @@
 
 def sspec():
     return pl.BlockSpec(memory_space=pltpu.SMEM)
-
-
-def aspec():
-    return pl.BlockSpec(memory_space=pl.ANY)
 
 
 def iota(shape, dim):
@@ -92,14 +88,11 @@
 
 
 def warp_kernel(offs, base, cols, frac, blend, *refs):
-    blocks, (pay, enc, S, MJ, MV, sems) = refs[:9], refs[9:]
+    blocks, (pay, enc, OWN, MJ, MV, sem) = refs[:9], refs[9:]
     core = lax.rem(lax.axis_index("rows"), 2)
     sign = 1 - 2 * core
-    copies = []
-    for k, off in enumerate(OFFSETS):
-        copies.append(pltpu.make_async_copy(blocks[k], S.at[4 + sign * off], sems.at[k]))
-    for copy in copies:
-        copy.start()
+    fetch = pltpu.make_async_copy(blocks[0], OWN, sem)
+    fetch.start()
     mats = []
     for j in range(4):
         lo, hi = max(j - 1, 0), min(j + 1, 3)
@@ -114,15 +107,20 @@
         target = cols[0, 0, 0, j] + x
         mat = jnp.where(src == target, 1.0 - q, 0.0) + jnp.where(src == target + 1, q, 0.0)
         mats.append(mat.astype(BF16))
-    for copy in copies:
-        copy.wait()
+    fetch.wait()
+    by_offset = dict(zip(OFFSETS, (OWN,) + tuple(blocks[1:])))
     for j in range(4):
         lo, hi = max(j - 1, 0), min(j + 1, 3)
         o = offs[0, 0, 0, j]
         for half in range(2):
-            window = S[o + 4 + half, :, lo * 128 : (hi + 1) * 128]
-            out = jnp.dot(window, mats[j], preferred_element_type=F32)
-            MJ[j, half * 128 : (half + 1) * 128, :] = out.astype(BF16).astype(F32)
+
+            def take(ref, j=j, lo=lo, hi=hi, half=half):
+                out = jnp.dot(ref[:, lo * 128 : (hi + 1) * 128], mats[j], preferred_element_type=F32)
+                MJ[j, half * 128 : (half + 1) * 128, :] = out.astype(BF16).astype(F32)
+
+            wanted = sign * (o + half)
+            for off in range(-4, 5):
+                pl.when(wanted == off)(lambda off=off: take(by_offset[off]))
     lane1 = iota((136, 128), 1)
     for pair in range(2):
         a = MJ[2 * pair, pl.ds(base[0, 0, 0, 2 * pair], 136), :]
@@ -154,23 +152,24 @@
 
 
 def make_warp(offs, base, cols, frac, blend, blocks):
+    own = pltpu.with_memory_space_constraint(blocks[0], pltpu.HBM)
     return pl.pallas_call(
         warp_kernel,
         out_shape=(
             jax.ShapeDtypeStruct((8, 24, 512), BF16),
             jax.ShapeDtypeStruct((128, 512), BF16),
         ),
-        in_specs=[sspec()] * 5 + [pl.BlockSpec(memory_space=pltpu.HBM)] + [aspec()] * 8,
+        in_specs=[sspec()] * 5 + [pl.BlockSpec(memory_space=pltpu.HBM)] + [vspec()] * 8,
         out_specs=(vspec(), vspec()),
         scratch_shapes=[
-            VMEM((9, 128, 512), BF16),
+            VMEM((128, 512), BF16),
             VMEM((4, 264, 128), F32),
             VMEM((136, 512), F32),
-            pltpu.SemaphoreType.DMA((9,)),
+            pltpu.SemaphoreType.DMA,
         ],
         compiler_params=pltpu.CompilerParams(vmem_limit_bytes=8 << 20),
         name="warp",
-    )(offs, base, cols, frac, blend, *blocks)
+    )(offs, base, cols, frac, blend, own, *blocks[1:])
 
 
 def prior_kernel(got, out, M):
@@ -198,124 +197,231 @@
     )(got)
 
 
-def encoder_kernel(enc, prior, inner, outer, w1, wd, wp, bb, out, AF, HE, HO, D, T, FS):
+def right(v):
+    at = iota(v.shape, 1)
+    return jnp.where(at == 0, 0.0, pltpu.roll(v, 1, 1))
+
+
+def left(v):
+    at = iota(v.shape, 1)
+    return jnp.where(at == 255, 0.0, pltpu.roll(v, 255, 1))
+
+
+def fill(AF, ch, tile, value):
+    even, odd = value[:, :256], value[:, 256:]
+    rows = pl.ds(16 * tile, 16)
+    AF[4 * ch, rows, :] = right(odd).astype(BF16)
+    AF[4 * ch + 1, rows, :] = even.astype(BF16)
+    AF[4 * ch + 2, rows, :] = odd.astype(BF16)
+    AF[4 * ch + 3, rows, :] = left(even).astype(BF16)
+
+
+def spread(bb, k, n):
+    return jnp.concatenate([bb[k]] * n, axis=0)
+
+
+def first_layer(AF, at, w1, bias, HE, HO, to):
+    data = AF[:, at : at + 32, :].reshape(256, 256)
+    for phase, H in enumerate((HE, HO)):
+        got = jnp.dot(w1[512 * phase : 512 * phase + 512, :], data, preferred_element_type=F32)
+        H[32 * to : 32 * to + 512, :] = jnp.maximum(got + bias, 0.0).astype(BF16)
+
+
+def down_layer(HE, HO, at, wd, bias, D, to):
+    even = jnp.dot(wd[0:96, 0:224], HE[32 * at : 32 * at + 224, :], preferred_element_type=F32)
+    odd = jnp.dot(wd[96:288, 0:224], HO[32 * at : 32 * at + 224, :], preferred_element_type=F32)
+    total = even + right(odd[0:96]) + odd[96:192] + bias
+    D[32 * to : 32 * to + 96, :] = jnp.maximum(total, 0.0).astype(BF16)
+
+
+def deep_sum(F, at, w, bias):
+    got = jnp.dot(w[...], F[32 * at : 32 * at + 256, :], preferred_element_type=F32)
+    return got[192:384] + right(got[0:192]) + left(got[384:576]) + bias
+
+
+def deep_layer(D, at, w, bias, T, to):
+    T[32 * to : 32 * to + 192, :] = jnp.maximum(deep_sum(D, at, w, bias), 0.0).astype(BF16)
+
+
+def last_layer(T, at, w, bias, FS, to):
+    total = deep_sum(T, at, w, bias)
+    for r in range(6):
+        for part in range(4):
+            for half in range(2):
+                FS[half, part, 8 * (to + r) : 8 * (to + r) + 8, :] = total[
+                    32 * r + 8 * part : 32 * r + 8 * part + 8, 128 * half : 128 * half + 128
+                ]
+
+
+def gather_rows(FS, start, count, O):
+    for ch in range(32):
+        for half in range(2):
+            O[ch, :, 128 * half : 128 * half + 128] = FS[
+                half, ch // 8, pl.ds(8 * start + ch % 8, count, stride=8), :
+            ].astype(BF16)
+
+
+def inner_kernel(enc, prior, w1, wd, wp, bb, out, keep_h, keep_d, keep_t, AF, HE, HO, D, T, FS, O, sem):
+    for k in range(8):
+        fill(AF, 0, k, enc[16 * k : 16 * k + 16, :].astype(F32))
+        fill(AF, 1, k, prior[k].astype(F32))
+    bias = spread(bb, 0, 16)
+    for g in range(7):
+        first_layer(AF, 16 * g, w1, bias, HE, HO, 16 * g)
+    for phase, H in enumerate((HE, HO)):
+        keep_h[phase, 0] = H[0:128, :]
+        keep_h[phase, 1] = H[3456:3584, :]
+    bias = spread(bb, 1, 3)
+    for g in range(18):
+        down_layer(HE, HO, 6 * g + 2, wd, bias, D, 3 * g)
+    keep_d[0] = D[0:256, :]
+    keep_d[1] = D[1472:1728, :]
+    bias = spread(bb, 2, 6)
+    for g in range(8):
+        deep_layer(D, 6 * g + 3, wp.at[0], bias, T, 6 * g)
+    keep_t[0] = T[0:384, :]
+    keep_t[1] = T[1152:1536, :]
+    bias = spread(bb, 3, 6)
+    for g in range(6):
+        last_layer(T, 6 * g, wp.at[1], bias, FS, 6 * g)
+    gather_rows(FS, 4, 32, O)
+    copy = pltpu.make_async_copy(O, out.at[0, 0, :, pl.ds(16, 32), :], sem)
+    copy.start()
+    copy.wait()
+
+
+def make_inner(enc, prior, w1, wd, wp, bb):
+    return pl.pallas_call(
+        inner_kernel,
+        out_shape=(
+            jax.ShapeDtypeStruct((1, 1, 32, 64, 256), BF16),
+            jax.ShapeDtypeStruct((2, 2, 128, 256), BF16),
+            jax.ShapeDtypeStruct((2, 256, 256), BF16),
+            jax.ShapeDtypeStruct((2, 384, 256), BF16),
+        ),
+        in_specs=[vspec()] * 6,
+        out_specs=(pl.BlockSpec(memory_space=pltpu.HBM), vspec(), vspec(), vspec()),
+        scratch_shapes=[
+            VMEM((8, 128, 256), BF16),
+            VMEM((3584, 256), BF16),
+            VMEM((3584, 256), BF16),
+            VMEM((1728, 256), BF16),
+            VMEM((1536, 256), BF16),
+            VMEM((2, 4, 288, 128), F32),
+            VMEM((32, 32, 256), BF16),
+            pltpu.SemaphoreType.DMA,
+        ],
+        compiler_params=pltpu.CompilerParams(vmem_limit_bytes=16 << 20),
+        cost_estimate=pl.CostEstimate(
+            flops=6_000_000_000, bytes_accessed=4_000_000, transcendentals=0
+        ),
+        name="middle",
+    )(enc, prior, w1, wd, wp, bb)
+
+
+def outer_kernel(
+    enc, prior, inner, outer, w1, wd, wp, bb, keep_h, keep_d, keep_t, got, out,
+    AF, HE, HO, D, T, FS, O, sems,
+):
     place = lax.axis_index("rows")
-    core = lax.rem(place, 2)
-    is_top = core == 0
-    lane = iota((16, 256), 1)
+    is_top = lax.rem(place, 2) == 0
     zeros8 = jnp.zeros((8, 512), F32)
-
-    def fill(ch, tile, value):
-        even, odd = value[:, :256], value[:, 256:]
-        rows = pl.ds(16 * tile, 16)
-        AF[4 * ch, rows, :] = jnp.where(lane == 0, 0.0, pltpu.roll(odd, 1, 1)).astype(BF16)
-        AF[4 * ch + 1, rows, :] = even.astype(BF16)
-        AF[4 * ch + 2, rows, :] = odd.astype(BF16)
-        AF[4 * ch + 3, rows, :] = jnp.where(lane == 255, 0.0, pltpu.roll(even, 255, 1)).astype(BF16)
-
     for ch in range(2):
         a = inner[ch].astype(F32)
         b = outer[ch].astype(F32)
         above = jnp.where(is_top, b[8:16], a[8:16])
         below = jnp.where(is_top, a[0:8], b[0:8])
-        fill(ch, 0, jnp.concatenate([zeros8, above], axis=0))
-        fill(ch, 9, jnp.concatenate([below, zeros8], axis=0))
-    for k in range(8):
-        fill(0, k + 1, enc[16 * k : 16 * k + 16, :].astype(F32))
-        fill(1, k + 1, prior[k].astype(F32))
-
-    def spread(k, n):
-        return jnp.concatenate([bb[k]] * n, axis=0)
-
-    bias16 = spread(0, 16)
-    for g in range(9):
-        data = AF[:, 16 * g : 16 * g + 32, :].reshape(256, 256)
-        for phase, H in enumerate((HE, HO)):
-            got = jnp.dot(w1[512 * phase : 512 * phase + 512, :], data, preferred_element_type=F32)
-            H[512 * g : 512 * g + 512, :] = jnp.maximum(got + bias16, 0.0).astype(BF16)
+        fill(AF.at[0], ch, 0, jnp.concatenate([zeros8, above], axis=0))
+        fill(AF.at[1], ch, 1, jnp.concatenate([below, zeros8], axis=0))
+    fill(AF.at[0], 0, 1, enc[0:16, :].astype(F32))
+    fill(AF.at[0], 1, 1, prior[0].astype(F32))
+    fill(AF.at[1], 0, 0, enc[112:128, :].astype(F32))
+    fill(AF.at[1], 1, 0, prior[7].astype(F32))
+    bias = spread(bb, 0, 16)
+    for phase, H in enumerate((HE, HO)):
+        H[0, 512:640, :] = keep_h[phase, 0]
+        H[1, 0:128, :] = keep_h[phase, 1]
+    first_layer(AF.at[0], 0, w1, bias, HE.at[0], HO.at[0], 0)
+    first_layer(AF.at[1], 0, w1, bias, HE.at[1], HO.at[1], 4)
 
     @pl.when(place == 0)
     def _():
-        HE[0:160, :] = jnp.zeros((160, 256), BF16)
-        HO[0:160, :] = jnp.zeros((160, 256), BF16)
+        HE[0, 0:160, :] = jnp.zeros((160, 256), BF16)
+        HO[0, 0:160, :] = jnp.zeros((160, 256), BF16)
 
     @pl.when(place == 31)
     def _():
-        HE[4256:4608, :] = jnp.zeros((352, 256), BF16)
-        HO[4256:4608, :] = jnp.zeros((352, 256), BF16)
-
-    def right(v):
-        at = iota(v.shape, 1)
-        return jnp.where(at == 0, 0.0, pltpu.roll(v, 1, 1))
-
-    def left(v):
-        at = iota(v.shape, 1)
-        return jnp.where(at == 255, 0.0, pltpu.roll(v, 255, 1))
-
-    bias3 = spread(1, 3)
-    for g in range(23):
-        even = jnp.dot(wd[0:96, 0:224], HE[192 * g : 192 * g + 224, :], preferred_element_type=F32)
-        odd = jnp.dot(wd[96:288, 0:224], HO[192 * g : 192 * g + 224, :], preferred_element_type=F32)
-        total = even + right(odd[0:96]) + odd[96:192] + bias3
-        D[96 * g : 96 * g + 96, :] = jnp.maximum(total, 0.0).astype(BF16)
+        HE[1, 288:640, :] = jnp.zeros((352, 256), BF16)
+        HO[1, 288:640, :] = jnp.zeros((352, 256), BF16)
+
+    bias = spread(bb, 1, 3)
+    D[0, 288:544, :] = keep_d[0]
+    D[1, 0:256, :] = keep_d[1]
+    for g in range(3):
+        down_layer(HE.at[0], HO.at[0], 6 * g, wd, bias, D.at[0], 3 * g)
+    for g in range(2):
+        down_layer(HE.at[1], HO.at[1], 6 * g + 2, wd, bias, D.at[1], 3 * g + 8)
 
     @pl.when(place == 0)
     def _():
-        D[0:64, :] = jnp.zeros((64, 256), BF16)
+        D[0, 0:64, :] = jnp.zeros((64, 256), BF16)
 
     @pl.when(place == 31)
     def _():
-        D[2112:2208, :] = jnp.zeros((96, 256), BF16)
-
-    bias6 = spread(2, 6)
-    for g in range(11):
-        got = jnp.dot(wp[0], D[192 * g : 192 * g + 256, :], preferred_element_type=F32)
-        total = got[192:384] + right(got[0:192]) + left(got[384:576]) + bias6
-        T[192 * g : 192 * g + 192, :] = jnp.maximum(total, 0.0).astype(BF16)
-    T[2112:2176, :] = jnp.zeros((64, 256), BF16)
+        D[1, 352:448, :] = jnp.zeros((96, 256), BF16)
+
+    bias = spread(bb, 2, 6)
+    T[0, 384:768, :] = keep_t[0]
+    T[1, 0:384, :] = keep_t[1]
+    for g in range(2):
+        deep_layer(D.at[0], 6 * g, wp.at[0], bias, T.at[0], 6 * g)
+    deep_layer(D.at[1], 5, wp.at[0], bias, T.at[1], 12)
+    T[1, 576:768, :] = jnp.zeros((192, 256), BF16)
 
     @pl.when(place == 0)
     def _():
-        T[0:32, :] = jnp.zeros((32, 256), BF16)
+        T[0, 0:32, :] = jnp.zeros((32, 256), BF16)
 
     @pl.when(place == 31)
     def _():
-        T[2080:2112, :] = jnp.zeros((32, 256), BF16)
-
-    bias7 = spread(3, 6)
-    for g in range(11):
-        got = jnp.dot(wp[1], T[192 * g : 192 * g + 256, :], preferred_element_type=F32)
-        total = got[192:384] + right(got[0:192]) + left(got[384:576]) + bias7
-        for r in range(6):
-            for part in range(4):
-                for half in range(2):
-                    FS[half, part, 48 * g + 8 * r : 48 * g + 8 * r + 8, :] = total[
-                        32 * r + 8 * part : 32 * r + 8 * part + 8, 128 * half : 128 * half + 128
-                    ]
-    for ch in range(32):
-        for half in range(2):
-            out[0, 0, ch, :, 128 * half : 128 * half + 128] = FS[
-                half, ch // 8, pl.ds(ch % 8, 64, stride=8), :
-            ].astype(BF16)
-
-
-def make_encoder(enc, prior, inner, outer, w1, wd, wp, bb):
+        T[1, 544:576, :] = jnp.zeros((32, 256), BF16)
+
+    bias = spread(bb, 3, 6)
+    copies = []
+    for side in range(2):
+        for g in range(3):
+            last_layer(T.at[side], 6 * g, wp.at[1], bias, FS.at[side], 6 * g)
+        gather_rows(FS.at[side], 0, 16, O.at[side])
+        copy = pltpu.make_async_copy(
+            O.at[side], out.at[0, 0, :, pl.ds(48 * side, 16), :], sems.at[side]
+        )
+        copy.start()
+        copies.append(copy)
+    for copy in copies:
+        copy.wait()
+
+
+def make_outer(enc, prior, inner, outer, w1, wd, wp, bb, keep_h, keep_d, keep_t, got):
+    hbm = pl.BlockSpec(memory_space=pltpu.HBM)
     return pl.pallas_call(
-        encoder_kernel,
+        outer_kernel,
         out_shape=jax.ShapeDtypeStruct((1, 1, 32, 64, 256), BF16),
-        in_specs=[vspec()] * 8,
-        out_specs=vspec(),
+        in_specs=[vspec()] * 11 + [hbm],
+        out_specs=hbm,
         scratch_shapes=[
-            VMEM((8, 160, 256), BF16),
-            VMEM((4608, 256), BF16),
-            VMEM((4608, 256), BF16),
-            VMEM((2208, 256), BF16),
-            VMEM((2176, 256), BF16),
-            VMEM((2, 4, 528, 128), F32),
+            VMEM((2, 8, 32, 256), BF16),
+            VMEM((2, 640, 256), BF16),
+            VMEM((2, 640, 256), BF16),
+            VMEM((2, 544, 256), BF16),
+            VMEM((2, 768, 256), BF16),
+            VMEM((2, 2, 4, 144, 128), F32),
+            VMEM((2, 32, 16, 256), BF16),
+            pltpu.SemaphoreType.DMA((2,)),
         ],
-        compiler_params=pltpu.CompilerParams(vmem_limit_bytes=20 << 20),
-        name="encoder",
-    )(enc, prior, inner, outer, w1, wd, wp, bb)
+        input_output_aliases={11: 0},
+        compiler_params=pltpu.CompilerParams(vmem_limit_bytes=16 << 20),
+        name="border",
+    )(enc, prior, inner, outer, w1, wd, wp, bb, keep_h, keep_d, keep_t, got)
 
 
 def pairs(target):
@@ -363,7 +469,10 @@
     )
     inner = send(edges, SWAP)
     outer = send(edges, ACROSS)
-    return make_encoder(enc, prior, inner, outer, w1, wd, wp, bb)
+    got, keep_h, keep_d, keep_t = make_inner(enc, prior, w1, wd, wp, bb)
+    return make_outer(
+        enc, prior, inner, outer, w1, wd, wp, bb, keep_h, keep_d, keep_t, got
+    )
 
 
 def solution(mesh):

time: 70.5 us -> 67.3 us (0.955)
  the two profiles are of different devices: /device:TPU:6 before, /device:TPU:7 now
where the time goes in v2:
time: 67.3 us; the launch traced here: 66.5 us
  starting transfers between devices  23.8 us (35%)
  blocking collectives  17.8 us (26%)
  Pallas kernels  12.4 us (18%)
  waiting for transfers between devices  10.9 us (16%)
  between operations  0.87 us (1%)
  local copies, waits for them, and re-layouts  0.68 us (1%)
    ppermute x10, starting transfers between devices, send(): return lax.ppermute(value, 'rows', route)  20.3 us
    all_to_all x1, blocking collectives, per_device(): got = lax.all_to_all(pay, 'gz', 0, 0)  17.8 us
    all_to_all x1, waiting for transfers between devices, per_device(): prior = lax.all_to_all(given, 'gz', 0, 0)  7.87 us
    pallas_call x1, Pallas kernels, make_inner(): pl.pallas_call(inner_kernel, out_shape=(jax.ShapeDtypeStruct((1, 1, 32, 6...  4.48 us
    all_to_all x1, starting transfers between devices, per_device(): prior = lax.all_to_all(given, 'gz', 0, 0)  3.52 us
    pallas_call x1, Pallas kernels, make_outer(): pl.pallas_call(outer_kernel, out_shape=jax.ShapeDtypeStruct((1, 1, 32, 64...  3.31 us
    pallas_call x1, Pallas kernels, make_warp(): pl.pallas_call(warp_kernel, out_shape=(jax.ShapeDtypeStruct((8, 24, 512),...  3.19 us
    ppermute x10, waiting for transfers between devices, send(): return lax.ppermute(value, 'rows', route)  3.07 us
  transfers between devices with their start and end apart: 11, of which 3 were waited for; matrix products, arithmetic and copies ran while one was open for 0% of the time, Pallas kernels for 8%

profile of v2, /device:TPU:7, one launch (start us, length us, event | category | flops | bytes accessed | tf_op | source)
XLA Modules:
  0.0 66.5 jit_solution(587961394110700191)
XLA Ops:
  0.0 3.3 %collective-permute-start.1 = (bf16[128,512]{1,0:T(8,128)(2,1)}, bf16[128,512]{1,0:T(8,128)(2,1)S(1)}, u32[]{:S(2)}, u32[]{:S(2)}) collective-permute-start(bf16[128,512]{1,0:T(8,128)(2,1)} %bitcast.15), channel_id=1, source_target_pairs={{1,3},{2,0},{3,5},{4,2},{5,7},{6,4},{7,9},{8,6},{9,11},{10,8},{11,... | collective-permute-start | bytes 393224 | tf_op jit(solution)/shard_map/ppermute | solution.py:443
  3.4 4.2 %collective-permute-start.3 = (bf16[128,512]{1,0:T(8,128)(2,1)}, bf16[128,512]{1,0:T(8,128)(2,1)S(1)}, u32[]{:S(2)}, u32[]{:S(2)}) collective-permute-start(bf16[128,512]{1,0:T(8,128)(2,1)} %bitcast.16), channel_id=1, source_target_pairs={{0,2},{2,4},{3,1},{4,6},{5,3},{6,8},{7,5},{8,10},{9,7},{10,12},{11... | collective-permute-start | bytes 393224 | tf_op jit(solution)/shard_map/ppermute | solution.py:443
  7.6 0.6 collective-permute-done.1.refs_2_
  8.2 1.9 %collective-permute-start.5 = (bf16[128,512]{1,0:T(8,128)(2,1)S(1)}, bf16[128,512]{1,0:T(8,128)(2,1)S(1)}, u32[]{:S(2)}, u32[]{:S(2)}) collective-permute-start(bf16[128,512]{1,0:T(8,128)(2,1)S(1)} %collective-permute-done.1.refs_2_), channel_id=1, source_target_pairs={{1,3},{2,0},{3,5},{4,2},{5,7},{6,4},{7,9},{8,6},{9,11},{10,8},{11,... | collective-permute-start | bytes 393224 | tf_op jit(solution)/shard_map/ppermute | solution.py:443
  10.1 5.2 %collective-permute-start = (bf16[128,512]{1,0:T(8,128)(2,1)}, bf16[128,512]{1,0:T(8,128)(2,1)S(1)}, u32[]{:S(2)}, u32[]{:S(2)}) collective-permute-start(bf16[128,512]{1,0:T(8,128)(2,1)} %bitcast.17), channel_id=1, source_target_pairs={{0,1},{1,0},{2,3},{3,2},{4,5},{5,4},{6,7},{7,6},{8,9},{9,8},{10,11... | collective-permute-start | bytes 393224 | tf_op jit(solution)/shard_map/ppermute | solution.py:443
  15.3 0.0 collective-permute-done.3.refs_4_
  15.3 1.9 %collective-permute-start.7 = (bf16[128,512]{1,0:T(8,128)(2,1)S(1)}, bf16[128,512]{1,0:T(8,128)(2,1)S(1)}, u32[]{:S(2)}, u32[]{:S(2)}) collective-permute-start(bf16[128,512]{1,0:T(8,128)(2,1)S(1)} %collective-permute-done.3.refs_4_), channel_id=1, source_target_pairs={{3,1},{5,3},{7,5},{9,7},{11,9},{13,11},{15,13},{17,15},{19,17},{21... | collective-permute-start | bytes 393224 | tf_op jit(solution)/shard_map/ppermute | solution.py:443
  17.2 0.1 collective-permute-start.4
  17.3 0.5 collective-permute-start.2
  17.8 0.0 collective-permute-done.5.refs_6_
  17.8 0.1 collective-permute-start.6
  18.6 0.0 collective-permute-done.refs_1_
  18.6 2.4 %collective-permute-done.7.refs_8_ = bf16[128,512]{1,0:T(8,128)(2,1)S(1)} collective-permute-done((bf16[128,512]{1,0:T(8,128)(2,1)S(1)}, bf16[128,512]{1,0:T(8,128)(2,1)S(1)}, u32[]{:S(2)}, u32[]{:S(2)}) %collective-permute-start.7) | collective-permute-done | bytes 131104 | tf_op jit(solution)/shard_map/ppermute | solution.py:443
  21.0 0.0 collective-permute-done.4.refs_5_
  21.0 0.0 collective-permute-done.2.refs_3_
  21.0 0.0 collective-permute-done.6.refs_7_
  21.1 3.2 %warp.1 = (bf16[8,24,512]{2,1,0:T(8,128)(2,1)S(1)}, bf16[128,512]{1,0:T(8,128)(2,1)S(1)}) custom-call(s32[1,1,1,4]{3,2,1,0:T(1,128)S(1)} %copy-done.5, s32[1,1,1,4]{3,2,1,0:T(1,128)S(1)} %copy-done.6, s32[1,1,1,4]{3,2,1,0:T(1,128)S(1)} %copy-done.7, s32[2,1,1,1,4]{4,3,2,1,0:T(1,128)S(1)} %copy-done.4, f32[1,1]{1,0:T(1,128)S(6)} %copy.15.blend, ...), custom_call_target="tpu_custom_call" | custom-call | tf_op jit(solution)/shard_map/warp/pallas_call | solution.py:156
  24.3 17.8 %all_to_all.10.got = bf16[8,24,512]{2,1,0:T(8,128)(2,1)S(1)} all-to-all(bf16[8,24,512]{2,1,0:T(8,128)(2,1)S(1)} %get-tuple-element.16), channel_id=1, replica_groups=mesh['gz'=8,'rows'=32] {'gz'}, dimensions={0} | all-to-all | bytes 393216 | tf_op jit(solution)/shard_map/all_to_all | solution.py:461
  42.0 0.8 %prior.1 = bf16[8,16,512]{2,1,0:T(8,128)(2,1)} custom-call(bf16[8,24,512]{2,1,0:T(8,128)(2,1)S(1)} %all_to_all.10.got), custom_call_target="tpu_custom_call" | custom-call | tf_op jit(solution)/shard_map/prior/pallas_call | solution.py:189
  42.8 3.5 %all-to-all-start.1 = ((bf16[8,16,512]{2,1,0:T(8,128)(2,1)}), bf16[8,16,512]{2,1,0:T(8,128)(2,1)S(1)}, u32[]{:S(2)}, u32[]{:S(2)}) async-start(bf16[8,16,512]{2,1,0:T(8,128)(2,1)} %prior.1), calls=%async_computation.1 | async-start | bytes 262144 | tf_op jit(solution)/shard_map/all_to_all | solution.py:463
  46.4 0.0 copy-start.2
  46.4 0.0 copy-start.3
  46.4 0.6 copy-done.2
  47.0 0.0 copy-done.3
  47.1 0.7 weights.1
  47.7 7.9 %all-to-all-done.1.prior = bf16[8,16,512]{2,1,0:T(8,128)(2,1)S(1)} async-done(((bf16[8,16,512]{2,1,0:T(8,128)(2,1)}), bf16[8,16,512]{2,1,0:T(8,128)(2,1)S(1)}, u32[]{:S(2)}, u32[]{:S(2)}) %all-to-all-start.1) | async-done | bytes 131104 | tf_op jit(solution)/shard_map/all_to_all | solution.py:463
  55.6 2.8 %collective-permute-start.9 = (bf16[2,16,512]{2,1,0:T(8,128)(2,1)S(1)}, bf16[2,16,512]{2,1,0:T(8,128)(2,1)S(1)}, u32[]{:S(2)}, u32[]{:S(2)}) collective-permute-start(bf16[2,16,512]{2,1,0:T(8,128)(2,1)S(1)} %pad_maximum_fusion), channel_id=1, source_target_pairs={{1,2},{2,1},{3,4},{4,3},{5,6},{6,5},{7,8},{8,7},{9,10},{10,9},{11,... | collective-permute-start | bytes 98312 | tf_op jit(solution)/shard_map/ppermute | solution.py:443
  58.4 0.3 collective-permute-start.8
  58.7 4.5 %middle.1 = (bf16[1,1,32,64,256]{4,3,2,1,0:T(8,128)(2,1)}, bf16[2,2,128,256]{3,2,1,0:T(8,128)(2,1)S(1)}, bf16[2,256,256]{2,1,0:T(8,128)(2,1)S(1)}, bf16[2,384,256]{2,1,0:T(8,128)(2,1)S(1)}) custom-call(bf16[128,512]{1,0:T(8,128)(2,1)S(1)} %get-tuple-element.15.enc, bf16[8,16,512]{2,1,0:T(8,128)(2,1)S(1)} %all-to-all-done.1.prior, ...), custom_call_target="tpu_custom_call" | custom-call | flops 6000000000 | bytes 4000000 | tf_op jit(solution)/shard_map/middle/pallas_call | solution.py:294
  63.2 0.0 collective-permute-done.9.outer
  63.2 0.0 collective-permute-done.8.inner
  63.2 3.3 %border.1 = bf16[1,1,32,64,256]{4,3,2,1,0:T(8,128)(2,1)} custom-call(bf16[128,512]{1,0:T(8,128)(2,1)S(1)} %get-tuple-element.15.enc, bf16[8,16,512]{2,1,0:T(8,128)(2,1)S(1)} %all-to-all-done.1.prior, bf16[2,16,512]{2,1,0:T(8,128)(2,1)S(1)} %collective-permute-done.8.inner, ...), custom_call_target="tpu_custom_call", output_to_operand_aliasing={{}: (11, {})} | custom-call | tf_op jit(solution)/shard_map/border/pallas_call | solution.py:406
  (20 shorter events, 0.1 us)
Async XLA Ops:
  0.0 21.0 %copy-start.6 = (s32[1,1,1,4]{3,2,1,0:T(1,128)S(1)}, s32[1,1,1,4]{3,2,1,0:T(1,128)}, u32[]{:S(2)}) copy-start(s32[1,1,1,4]{3,2,1,0:T(1,128)} %base.1) | copy-start | bytes 52
  0.0 21.1 %copy-start.7 = (s32[1,1,1,4]{3,2,1,0:T(1,128)S(1)}, s32[1,1,1,4]{3,2,1,0:T(1,128)}, u32[]{:S(2)}) copy-start(s32[1,1,1,4]{3,2,1,0:T(1,128)} %cols.1) | copy-start | bytes 52
  0.0 21.1 %copy-start.4 = (s32[2,1,1,1,4]{4,3,2,1,0:T(1,128)S(1)}, s32[2,1,1,1,4]{4,3,2,1,0:T(1,128)}, u32[]{:S(2)}) copy-start(s32[2,1,1,1,4]{4,3,2,1,0:T(1,128)} %frac.1) | copy-start | bytes 100
  0.0 21.1 %copy-start.5 = (s32[1,1,1,4]{3,2,1,0:T(1,128)S(1)}, s32[1,1,1,4]{3,2,1,0:T(1,128)}, u32[]{:S(2)}) copy-start(s32[1,1,1,4]{3,2,1,0:T(1,128)} %offs.1) | copy-start | bytes 52
  0.0 8.2 %collective-permute-start.1 = (bf16[128,512]{1,0:T(8,128)(2,1)}, bf16[128,512]{1,0:T(8,128)(2,1)S(1)}, u32[]{:S(2)}, u32[]{:S(2)}) collective-permute-start(bf16[128,512]{1,0:T(8,128)(2,1)} %bitcast.15), channel_id=1, source_target_pairs={{1,3},{2,0},{3,5},{4,2},{5,7},{6,4},{7,9},{8,6},{9,11},{10,8},{11,... | collective-permute-start | bytes 393224 | tf_op jit(solution)/shard_map/ppermute | solution.py:443
  3.4 12.0 %collective-permute-start.3 = (bf16[128,512]{1,0:T(8,128)(2,1)}, bf16[128,512]{1,0:T(8,128)(2,1)S(1)}, u32[]{:S(2)}, u32[]{:S(2)}) collective-permute-start(bf16[128,512]{1,0:T(8,128)(2,1)} %bitcast.16), channel_id=1, source_target_pairs={{0,2},{2,4},{3,1},{4,6},{5,3},{6,8},{7,5},{8,10},{9,7},{10,12},{11... | collective-permute-start | bytes 393224 | tf_op jit(solution)/shard_map/ppermute | solution.py:443
  8.2 9.7 %collective-permute-start.5 = (bf16[128,512]{1,0:T(8,128)(2,1)S(1)}, bf16[128,512]{1,0:T(8,128)(2,1)S(1)}, u32[]{:S(2)}, u32[]{:S(2)}) collective-permute-start(bf16[128,512]{1,0:T(8,128)(2,1)S(1)} %collective-permute-done.1.refs_2_), channel_id=1, source_target_pairs={{1,3},{2,0},{3,5},{4,2},{5,7},{6,4},{7,9},{8,6},{9,11},{10,8},{11,... | collective-permute-start | bytes 393224 | tf_op jit(solution)/shard_map/ppermute | solution.py:443
  10.1 8.5 %collective-permute-start = (bf16[128,512]{1,0:T(8,128)(2,1)}, bf16[128,512]{1,0:T(8,128)(2,1)S(1)}, u32[]{:S(2)}, u32[]{:S(2)}) collective-permute-start(bf16[128,512]{1,0:T(8,128)(2,1)} %bitcast.17), channel_id=1, source_target_pairs={{0,1},{1,0},{2,3},{3,2},{4,5},{5,4},{6,7},{7,6},{8,9},{9,8},{10,11... | collective-permute-start | bytes 393224 | tf_op jit(solution)/shard_map/ppermute | solution.py:443
  15.3 5.7 %collective-permute-start.7 = (bf16[128,512]{1,0:T(8,128)(2,1)S(1)}, bf16[128,512]{1,0:T(8,128)(2,1)S(1)}, u32[]{:S(2)}, u32[]{:S(2)}) collective-permute-start(bf16[128,512]{1,0:T(8,128)(2,1)S(1)} %collective-permute-done.3.refs_4_), channel_id=1, source_target_pairs={{3,1},{5,3},{7,5},{9,7},{11,9},{13,11},{15,13},{17,15},{19,17},{21... | collective-permute-start | bytes 393224 | tf_op jit(solution)/shard_map/ppermute | solution.py:443
  17.2 3.8 %collective-permute-start.4 = (bf16[128,512]{1,0:T(8,128)(2,1)S(1)}, bf16[128,512]{1,0:T(8,128)(2,1)S(1)}, u32[]{:S(2)}, u32[]{:S(2)}) collective-permute-start(bf16[128,512]{1,0:T(8,128)(2,1)S(1)} %collective-permute-done.3.refs_4_), channel_id=1, source_target_pairs={{0,1},{1,0},{2,3},{3,2},{4,5},{5,4},{6,7},{7,6},{8,9},{9,8},{10,11... | collective-permute-start | bytes 393224 | tf_op jit(solution)/shard_map/ppermute | solution.py:443
  17.3 3.7 %collective-permute-start.2 = (bf16[128,512]{1,0:T(8,128)(2,1)S(1)}, bf16[128,512]{1,0:T(8,128)(2,1)S(1)}, u32[]{:S(2)}, u32[]{:S(2)}) collective-permute-start(bf16[128,512]{1,0:T(8,128)(2,1)S(1)} %collective-permute-done.1.refs_2_), channel_id=1, source_target_pairs={{0,1},{1,0},{2,3},{3,2},{4,5},{5,4},{6,7},{7,6},{8,9},{9,8},{10,11... | collective-permute-start | bytes 393224 | tf_op jit(solution)/shard_map/ppermute | solution.py:443
  17.8 3.2 %collective-permute-start.6 = (bf16[128,512]{1,0:T(8,128)(2,1)S(1)}, bf16[128,512]{1,0:T(8,128)(2,1)S(1)}, u32[]{:S(2)}, u32[]{:S(2)}) collective-permute-start(bf16[128,512]{1,0:T(8,128)(2,1)S(1)} %collective-permute-done.5.refs_6_), channel_id=1, source_target_pairs={{0,1},{1,0},{2,3},{3,2},{4,5},{5,4},{6,7},{7,6},{8,9},{9,8},{10,11... | collective-permute-start | bytes 393224 | tf_op jit(solution)/shard_map/ppermute | solution.py:443
  42.8 3.6 %copy-start = (bf16[2,9,32,32]{3,2,1,0:T(8,128)(2,1)S(1)}, bf16[2,9,32,32]{3,2,1,0:T(8,128)(2,1)}, u32[]{:S(2)}) copy-start(bf16[2,9,32,32]{3,2,1,0:T(8,128)(2,1)} %kp.1) | copy-start | bytes 110596
  42.8 3.6 %copy-start.1 = (bf16[9,32,32]{2,1,0:T(8,128)(2,1)S(1)}, bf16[9,32,32]{2,1,0:T(8,128)(2,1)}, u32[]{:S(2)}) copy-start(bf16[9,32,32]{2,1,0:T(8,128)(2,1)} %kd.1) | copy-start | bytes 55300
  42.8 3.6 %copy-start.8 = (f32[32]{0:T(128)S(1)}, f32[32]{0:T(128)}, u32[]{:S(2)}) copy-start(f32[32]{0:T(128)} %param.19) | copy-start | bytes 388
  42.8 3.6 %copy-start.9 = (f32[32]{0:T(128)S(1)}, f32[32]{0:T(128)}, u32[]{:S(2)}) copy-start(f32[32]{0:T(128)} %param.21) | copy-start | bytes 388
  42.8 12.8 %all-to-all-start.1 = ((bf16[8,16,512]{2,1,0:T(8,128)(2,1)}), bf16[8,16,512]{2,1,0:T(8,128)(2,1)S(1)}, u32[]{:S(2)}, u32[]{:S(2)}) async-start(bf16[8,16,512]{2,1,0:T(8,128)(2,1)} %prior.1), calls=%async_computation.1 | async-start | bytes 262144 | tf_op jit(solution)/shard_map/all_to_all | solution.py:463
  46.4 0.7 %copy-start.2 = (bf16[9,32,2]{1,2,0:T(2,128)(2,1)S(1)}, bf16[9,32,2]{1,2,0:T(2,128)(2,1)}, u32[]{:S(2)}) copy-start(bf16[9,32,2]{1,2,0:T(2,128)(2,1)} %param.18) | copy-start | bytes 3460
  46.4 0.7 %copy-start.3 = (f32[2,32]{1,0:T(2,128)S(1)}, f32[2,32]{1,0:T(2,128)}, u32[]{:S(2)}) copy-start(f32[2,32]{1,0:T(2,128)} %bp.1) | copy-start | bytes 772
  55.6 7.6 %collective-permute-start.9 = (bf16[2,16,512]{2,1,0:T(8,128)(2,1)S(1)}, bf16[2,16,512]{2,1,0:T(8,128)(2,1)S(1)}, u32[]{:S(2)}, u32[]{:S(2)}) collective-permute-start(bf16[2,16,512]{2,1,0:T(8,128)(2,1)S(1)} %pad_maximum_fusion), channel_id=1, source_target_pairs={{1,2},{2,1},{3,4},{4,3},{5,6},{6,5},{7,8},{8,7},{9,10},{10,9},{11,... | collective-permute-start | bytes 98312 | tf_op jit(solution)/shard_map/ppermute | solution.py:443
  58.4 4.8 %collective-permute-start.8 = (bf16[2,16,512]{2,1,0:T(8,128)(2,1)S(1)}, bf16[2,16,512]{2,1,0:T(8,128)(2,1)S(1)}, u32[]{:S(2)}, u32[]{:S(2)}) collective-permute-start(bf16[2,16,512]{2,1,0:T(8,128)(2,1)S(1)} %pad_maximum_fusion), channel_id=1, source_target_pairs={{0,1},{1,0},{2,3},{3,2},{4,5},{5,4},{6,7},{7,6},{8,9},{9,8},{10,11... | collective-permute-start | bytes 98312 | tf_op jit(solution)/shard_map/ppermute | solution.py:443

commit v3 on v2

--- a/solution.py
+++ b/solution.py
@@ -88,11 +88,14 @@
 
 
 def warp_kernel(offs, base, cols, frac, blend, *refs):
-    blocks, (pay, enc, OWN, MJ, MV, sem) = refs[:9], refs[9:]
+    blocks, (pay, enc, S, MJ, MV, sem) = refs[:9], refs[9:]
     core = lax.rem(lax.axis_index("rows"), 2)
     sign = 1 - 2 * core
-    fetch = pltpu.make_async_copy(blocks[0], OWN, sem)
+    fetch = pltpu.make_async_copy(blocks[0], S.at[4], sem)
     fetch.start()
+    for k, off in enumerate(OFFSETS):
+        if k > 0:
+            S[4 + sign * off] = blocks[k][...]
     mats = []
     for j in range(4):
         lo, hi = max(j - 1, 0), min(j + 1, 3)
@@ -108,19 +111,12 @@
         mat = jnp.where(src == target, 1.0 - q, 0.0) + jnp.where(src == target + 1, q, 0.0)
         mats.append(mat.astype(BF16))
     fetch.wait()
-    by_offset = dict(zip(OFFSETS, (OWN,) + tuple(blocks[1:])))
     for j in range(4):
         lo, hi = max(j - 1, 0), min(j + 1, 3)
-        o = offs[0, 0, 0, j]
-        for half in range(2):
-
-            def take(ref, j=j, lo=lo, hi=hi, half=half):
-                out = jnp.dot(ref[:, lo * 128 : (hi + 1) * 128], mats[j], preferred_element_type=F32)
-                MJ[j, half * 128 : (half + 1) * 128, :] = out.astype(BF16).astype(F32)
-
-            wanted = sign * (o + half)
-            for off in range(-4, 5):
-                pl.when(wanted == off)(lambda off=off: take(by_offset[off]))
+        first = offs[0, 0, 0, j] + 4
+        window = S[pl.ds(first, 2), :, lo * 128 : (hi + 1) * 128].reshape(256, (hi - lo + 1) * 128)
+        out = jnp.dot(window, mats[j], preferred_element_type=F32)
+        MJ[j, 0:256, :] = out.astype(BF16).astype(F32)
     lane1 = iota((136, 128), 1)
     for pair in range(2):
         a = MJ[2 * pair, pl.ds(base[0, 0, 0, 2 * pair], 136), :]
@@ -130,25 +126,29 @@
             jnp.where(lane1 < 64, b, a), 64, 1
         )
     lane = iota((8, 512), 1)
-    row = iota((8, 512), 0)
     which = (lane >> 6) & 3
     p = jnp.zeros((8, 512), F32)
     for j in range(4):
         p = jnp.where(which == j, frac[0, 0, 0, 0, j].astype(F32) * (1.0 / 256.0), p)
-    rate = jnp.full((8, 512), blend[0, 0], F32)
+    rate = jnp.full((16, 128), blend[0, 0], F32)
     top = rate.astype(BF16).astype(F32)
     mid = (rate - top).astype(BF16).astype(F32)
     low = rate - top - mid
-    extra = jnp.where(row == 1, p, jnp.where(row == 2, top, jnp.where(row == 3, mid, low)))
-    extra = jnp.where(row > 4, 0.0, extra)
+    row = iota((16, 128), 0)
+    extra = jnp.where(row == 8, top, jnp.where(row == 9, mid, jnp.where(row == 10, low, 0.0)))
+    for c in range(4):
+        extra = jnp.where(row == 4 + c, p[0:1, 128 * c : 128 * c + 128], extra)
     p16 = jnp.concatenate([p, p], axis=0)
     for k in range(8):
         here = MV[16 * k : 16 * k + 16, :]
         below = MV[16 * k + 1 : 16 * k + 17, :]
         enc[16 * k : 16 * k + 16, :] = ((1.0 - p16) * here + p16 * below).astype(BF16)
-        pay[k, 0:16, :] = here.astype(BF16)
-        tail = MV[16 * k + 16 : 16 * k + 24, :]
-        pay[k, 16:24, :] = jnp.where(row == 0, tail, extra).astype(BF16)
+        pay[k, :, 0:512] = here.astype(BF16)
+        tail = extra
+        for c in range(4):
+            piece = MV[16 * k + 16 : 16 * k + 17, 128 * c : 128 * c + 128]
+            tail = jnp.where(row == c, piece, tail)
+        pay[k, :, 512:640] = tail.astype(BF16)
 
 
 def make_warp(offs, base, cols, frac, blend, blocks):
@@ -156,13 +156,13 @@
     return pl.pallas_call(
         warp_kernel,
         out_shape=(
-            jax.ShapeDtypeStruct((8, 24, 512), BF16),
+            jax.ShapeDtypeStruct((8, 16, 640), BF16),
             jax.ShapeDtypeStruct((128, 512), BF16),
         ),
         in_specs=[sspec()] * 5 + [pl.BlockSpec(memory_space=pltpu.HBM)] + [vspec()] * 8,
         out_specs=(vspec(), vspec()),
         scratch_shapes=[
-            VMEM((128, 512), BF16),
+            VMEM((9, 128, 512), BF16),
             VMEM((4, 264, 128), F32),
             VMEM((136, 512), F32),
             pltpu.SemaphoreType.DMA,
@@ -178,9 +178,12 @@
         out[s] = state.astype(BF16)
         if s == 7:
             break
-        M[s] = got[s].astype(F32)
-        p = M[s, 17:18, :]
-        rate = M[s, 18:19, :] + M[s, 19:20, :] + M[s, 20:21, :]
+        M[s, 0:16, :] = got[s, :, 0:512].astype(F32)
+        extra = got[s, :, 512:640].astype(F32)
+        for c in range(4):
+            M[s, 16:17, 128 * c : 128 * c + 128] = extra[c : c + 1, :]
+        p = jnp.concatenate([extra[4 + c : 5 + c, :] for c in range(4)], axis=1)
+        rate = extra[8:9, 0:1] + extra[9:10, 0:1] + extra[10:11, 0:1]
         warped = (1.0 - p) * M[s, 0:16, :] + p * M[s, 1:17, :]
         state = rate * state + (1.0 - rate) * warped
 
@@ -220,18 +223,28 @@
     return jnp.concatenate([bb[k]] * n, axis=0)
 
 
-def first_layer(AF, at, w1, bias, HE, HO, to):
+def store(ref, at, value, mask):
+    if mask is not None:
+        scale, start, stop = mask
+        value = jnp.concatenate(
+            [part for part in (value[:start], value[start:stop] * scale, value[stop:]) if part.shape[0]],
+            axis=0,
+        )
+    ref[at : at + value.shape[0], :] = value.astype(BF16)
+
+
+def first_layer(AF, at, w1, bias, HE, HO, to, mask=None):
     data = AF[:, at : at + 32, :].reshape(256, 256)
     for phase, H in enumerate((HE, HO)):
         got = jnp.dot(w1[512 * phase : 512 * phase + 512, :], data, preferred_element_type=F32)
-        H[32 * to : 32 * to + 512, :] = jnp.maximum(got + bias, 0.0).astype(BF16)
-
-
-def down_layer(HE, HO, at, wd, bias, D, to):
+        store(H, 32 * to, jnp.maximum(got + bias, 0.0), mask)
+
+
+def down_layer(HE, HO, at, wd, bias, D, to, mask=None):
     even = jnp.dot(wd[0:96, 0:224], HE[32 * at : 32 * at + 224, :], preferred_element_type=F32)
     odd = jnp.dot(wd[96:288, 0:224], HO[32 * at : 32 * at + 224, :], preferred_element_type=F32)
     total = even + right(odd[0:96]) + odd[96:192] + bias
-    D[32 * to : 32 * to + 96, :] = jnp.maximum(total, 0.0).astype(BF16)
+    store(D, 32 * to, jnp.maximum(total, 0.0), mask)
 
 
 def deep_sum(F, at, w, bias):
@@ -239,8 +252,8 @@
     return got[192:384] + right(got[0:192]) + left(got[384:576]) + bias
 
 
-def deep_layer(D, at, w, bias, T, to):
-    T[32 * to : 32 * to + 192, :] = jnp.maximum(deep_sum(D, at, w, bias), 0.0).astype(BF16)
+def deep_layer(D, at, w, bias, T, to, mask=None):
+    store(T, 32 * to, jnp.maximum(deep_sum(D, at, w, bias), 0.0), mask)
 
 
 def last_layer(T, at, w, bias, FS, to):
@@ -261,7 +274,7 @@
             ].astype(BF16)
 
 
-def inner_kernel(enc, prior, w1, wd, wp, bb, out, keep_h, keep_d, keep_t, AF, HE, HO, D, T, FS, O, sem):
+def inner_kernel(enc, prior, w1, wd, wp, bb, O, keep_h, keep_d, keep_t, AF, HE, HO, D, T, FS):
     for k in range(8):
         fill(AF, 0, k, enc[16 * k : 16 * k + 16, :].astype(F32))
         fill(AF, 1, k, prior[k].astype(F32))
@@ -285,22 +298,19 @@
     for g in range(6):
         last_layer(T, 6 * g, wp.at[1], bias, FS, 6 * g)
     gather_rows(FS, 4, 32, O)
-    copy = pltpu.make_async_copy(O, out.at[0, 0, :, pl.ds(16, 32), :], sem)
-    copy.start()
-    copy.wait()
 
 
 def make_inner(enc, prior, w1, wd, wp, bb):
     return pl.pallas_call(
         inner_kernel,
         out_shape=(
-            jax.ShapeDtypeStruct((1, 1, 32, 64, 256), BF16),
+            jax.ShapeDtypeStruct((32, 32, 256), BF16),
             jax.ShapeDtypeStruct((2, 2, 128, 256), BF16),
             jax.ShapeDtypeStruct((2, 256, 256), BF16),
             jax.ShapeDtypeStruct((2, 384, 256), BF16),
         ),
         in_specs=[vspec()] * 6,
-        out_specs=(pl.BlockSpec(memory_space=pltpu.HBM), vspec(), vspec(), vspec()),
+        out_specs=(vspec(),) * 4,
         scratch_shapes=[
             VMEM((8, 128, 256), BF16),
             VMEM((3584, 256), BF16),
@@ -308,8 +318,6 @@
             VMEM((1728, 256), BF16),
             VMEM((1536, 256), BF16),
             VMEM((2, 4, 288, 128), F32),
-            VMEM((32, 32, 256), BF16),
-            pltpu.SemaphoreType.DMA,
         ],
         compiler_params=pltpu.CompilerParams(vmem_limit_bytes=16 << 20),
         cost_estimate=pl.CostEstimate(
@@ -323,8 +331,12 @@
     enc, prior, inner, outer, w1, wd, wp, bb, keep_h, keep_d, keep_t, got, out,
     AF, HE, HO, D, T, FS, O, sems,
 ):
+    copies = [pltpu.make_async_copy(got, out.at[0, 0, :, pl.ds(16, 32), :], sems.at[2])]
+    copies[0].start()
     place = lax.axis_index("rows")
     is_top = lax.rem(place, 2) == 0
+    keep_first = jnp.where(place == 0, 0.0, 1.0)
+    keep_last = jnp.where(place == 31, 0.0, 1.0)
     zeros8 = jnp.zeros((8, 512), F32)
     for ch in range(2):
         a = inner[ch].astype(F32)
@@ -341,53 +353,26 @@
     for phase, H in enumerate((HE, HO)):
         H[0, 512:640, :] = keep_h[phase, 0]
         H[1, 0:128, :] = keep_h[phase, 1]
-    first_layer(AF.at[0], 0, w1, bias, HE.at[0], HO.at[0], 0)
-    first_layer(AF.at[1], 0, w1, bias, HE.at[1], HO.at[1], 4)
-
-    @pl.when(place == 0)
-    def _():
-        HE[0, 0:160, :] = jnp.zeros((160, 256), BF16)
-        HO[0, 0:160, :] = jnp.zeros((160, 256), BF16)
-
-    @pl.when(place == 31)
-    def _():
-        HE[1, 288:640, :] = jnp.zeros((352, 256), BF16)
-        HO[1, 288:640, :] = jnp.zeros((352, 256), BF16)
-
+    first_layer(AF.at[0], 0, w1, bias, HE.at[0], HO.at[0], 0, (keep_first, 0, 160))
+    first_layer(AF.at[1], 0, w1, bias, HE.at[1], HO.at[1], 4, (keep_last, 160, 512))
     bias = spread(bb, 1, 3)
     D[0, 288:544, :] = keep_d[0]
     D[1, 0:256, :] = keep_d[1]
     for g in range(3):
-        down_layer(HE.at[0], HO.at[0], 6 * g, wd, bias, D.at[0], 3 * g)
+        mask = (keep_first, 0, 64) if g == 0 else None
+        down_layer(HE.at[0], HO.at[0], 6 * g, wd, bias, D.at[0], 3 * g, mask)
     for g in range(2):
-        down_layer(HE.at[1], HO.at[1], 6 * g + 2, wd, bias, D.at[1], 3 * g + 8)
-
-    @pl.when(place == 0)
-    def _():
-        D[0, 0:64, :] = jnp.zeros((64, 256), BF16)
-
-    @pl.when(place == 31)
-    def _():
-        D[1, 352:448, :] = jnp.zeros((96, 256), BF16)
-
+        mask = (keep_last, 0, 96) if g == 1 else None
+        down_layer(HE.at[1], HO.at[1], 6 * g + 2, wd, bias, D.at[1], 3 * g + 8, mask)
     bias = spread(bb, 2, 6)
     T[0, 384:768, :] = keep_t[0]
     T[1, 0:384, :] = keep_t[1]
     for g in range(2):
-        deep_layer(D.at[0], 6 * g, wp.at[0], bias, T.at[0], 6 * g)
-    deep_layer(D.at[1], 5, wp.at[0], bias, T.at[1], 12)
+        mask = (keep_first, 0, 32) if g == 0 else None
+        deep_layer(D.at[0], 6 * g, wp.at[0], bias, T.at[0], 6 * g, mask)
+    deep_layer(D.at[1], 5, wp.at[0], bias, T.at[1], 12, (keep_last, 160, 192))
     T[1, 576:768, :] = jnp.zeros((192, 256), BF16)
-
-    @pl.when(place == 0)
-    def _():
-        T[0, 0:32, :] = jnp.zeros((32, 256), BF16)
-
-    @pl.when(place == 31)
-    def _():
-        T[1, 544:576, :] = jnp.zeros((32, 256), BF16)
-
     bias = spread(bb, 3, 6)
-    copies = []
     for side in range(2):
         for g in range(3):
             last_layer(T.at[side], 6 * g, wp.at[1], bias, FS.at[side], 6 * g)
@@ -406,7 +391,7 @@
     return pl.pallas_call(
         outer_kernel,
         out_shape=jax.ShapeDtypeStruct((1, 1, 32, 64, 256), BF16),
-        in_specs=[vspec()] * 11 + [hbm],
+        in_specs=[vspec()] * 12,
         out_specs=hbm,
         scratch_shapes=[
             VMEM((2, 8, 32, 256), BF16),
@@ -416,9 +401,8 @@
             VMEM((2, 768, 256), BF16),
             VMEM((2, 2, 4, 144, 128), F32),
             VMEM((2, 32, 16, 256), BF16),
-            pltpu.SemaphoreType.DMA((2,)),
+            pltpu.SemaphoreType.DMA((3,)),
         ],
-        input_output_aliases={11: 0},
         compiler_params=pltpu.CompilerParams(vmem_limit_bytes=16 << 20),
         name="border",
     )(enc, prior, inner, outer, w1, wd, wp, bb, keep_h, keep_d, keep_t, got)

time: 67.3 us -> 64.2 us (0.954)
  Pallas kernels: 12.4 us -> 9.87 us
  blocking collectives: 17.8 us -> 17.1 us
    pallas_call x2, Pallas kernels: 7.67 us -> 5.61 us  [the longest x1 3.67 us: make_inner(): pl.pallas_call(inner_kernel, out_shape=(jax.ShapeDtypeStruct((32, 32, 256...]
    all_to_all x1, blocking collectives: 17.8 us -> 17.1 us  [per_device(): got = lax.all_to_all(pay, 'gz', 0, 0)]
  transfers between devices with their start and end apart: 11 -> 11, of which waited for: 3 -> 3; matrix products, arithmetic and copies ran while one was open for 0% -> 0% of each run, Pallas kernels for 8% -> 7%
where the time goes in v3:
time: 64.2 us; the launch traced here: 63.2 us
  starting transfers between devices  23.5 us (37%)
  blocking collectives  17.1 us (27%)
  waiting for transfers between devices  11.2 us (17%)
  Pallas kernels  9.87 us (15%)
  between operations  0.87 us (1%)
  local copies, waits for them, and re-layouts  0.68 us (1%)
    ppermute x10, starting transfers between devices, send(): return lax.ppermute(value, 'rows', route)  20 us
    all_to_all x1, blocking collectives, per_device(): got = lax.all_to_all(pay, 'gz', 0, 0)  17.1 us
    all_to_all x1, waiting for transfers between devices, per_device(): prior = lax.all_to_all(given, 'gz', 0, 0)  8.11 us
    pallas_call x1, Pallas kernels, make_inner(): pl.pallas_call(inner_kernel, out_shape=(jax.ShapeDtypeStruct((32, 32, 256...  3.67 us
    all_to_all x1, starting transfers between devices, per_device(): prior = lax.all_to_all(given, 'gz', 0, 0)  3.52 us
    ppermute x10, waiting for transfers between devices, send(): return lax.ppermute(value, 'rows', route)  3.07 us
    pallas_call x1, Pallas kernels, make_outer(): pl.pallas_call(outer_kernel, out_shape=jax.ShapeDtypeStruct((1, 1, 32, 64...  2.82 us
    pallas_call x1, Pallas kernels, make_warp(): pl.pallas_call(warp_kernel, out_shape=(jax.ShapeDtypeStruct((8, 16, 640),...  1.94 us
  transfers between devices with their start and end apart: 11, of which 3 were waited for; matrix products, arithmetic and copies ran while one was open for 0% of the time, Pallas kernels for 7%

profile of v3, /device:TPU:7, one launch (start us, length us, event | category | flops | bytes accessed | tf_op | source)
XLA Modules:
  0.0 63.2 jit_solution(16004075248741977970)
XLA Ops:
  0.0 3.3 %collective-permute-start.1 = (bf16[128,512]{1,0:T(8,128)(2,1)}, bf16[128,512]{1,0:T(8,128)(2,1)S(1)}, u32[]{:S(2)}, u32[]{:S(2)}) collective-permute-start(bf16[128,512]{1,0:T(8,128)(2,1)} %bitcast.15), channel_id=1, source_target_pairs={{1,3},{2,0},{3,5},{4,2},{5,7},{6,4},{7,9},{8,6},{9,11},{10,8},{11,... | collective-permute-start | bytes 393224 | tf_op jit(solution)/shard_map/ppermute | solution.py:427
  3.4 4.2 %collective-permute-start.3 = (bf16[128,512]{1,0:T(8,128)(2,1)}, bf16[128,512]{1,0:T(8,128)(2,1)S(1)}, u32[]{:S(2)}, u32[]{:S(2)}) collective-permute-start(bf16[128,512]{1,0:T(8,128)(2,1)} %bitcast.16), channel_id=1, source_target_pairs={{0,2},{2,4},{3,1},{4,6},{5,3},{6,8},{7,5},{8,10},{9,7},{10,12},{11... | collective-permute-start | bytes 393224 | tf_op jit(solution)/shard_map/ppermute | solution.py:427
  7.6 0.6 collective-permute-done.1.refs_2_
  8.2 1.9 %collective-permute-start.5 = (bf16[128,512]{1,0:T(8,128)(2,1)S(1)}, bf16[128,512]{1,0:T(8,128)(2,1)S(1)}, u32[]{:S(2)}, u32[]{:S(2)}) collective-permute-start(bf16[128,512]{1,0:T(8,128)(2,1)S(1)} %collective-permute-done.1.refs_2_), channel_id=1, source_target_pairs={{1,3},{2,0},{3,5},{4,2},{5,7},{6,4},{7,9},{8,6},{9,11},{10,8},{11,... | collective-permute-start | bytes 393224 | tf_op jit(solution)/shard_map/ppermute | solution.py:427
  10.1 5.2 %collective-permute-start = (bf16[128,512]{1,0:T(8,128)(2,1)}, bf16[128,512]{1,0:T(8,128)(2,1)S(1)}, u32[]{:S(2)}, u32[]{:S(2)}) collective-permute-start(bf16[128,512]{1,0:T(8,128)(2,1)} %bitcast.17), channel_id=1, source_target_pairs={{0,1},{1,0},{2,3},{3,2},{4,5},{5,4},{6,7},{7,6},{8,9},{9,8},{10,11... | collective-permute-start | bytes 393224 | tf_op jit(solution)/shard_map/ppermute | solution.py:427
  15.3 0.0 collective-permute-done.3.refs_4_
  15.3 1.9 %collective-permute-start.7 = (bf16[128,512]{1,0:T(8,128)(2,1)S(1)}, bf16[128,512]{1,0:T(8,128)(2,1)S(1)}, u32[]{:S(2)}, u32[]{:S(2)}) collective-permute-start(bf16[128,512]{1,0:T(8,128)(2,1)S(1)} %collective-permute-done.3.refs_4_), channel_id=1, source_target_pairs={{3,1},{5,3},{7,5},{9,7},{11,9},{13,11},{15,13},{17,15},{19,17},{21... | collective-permute-start | bytes 393224 | tf_op jit(solution)/shard_map/ppermute | solution.py:427
  17.2 0.1 collective-permute-start.4
  17.3 0.5 collective-permute-start.2
  17.8 0.0 collective-permute-done.5.refs_6_
  17.8 0.1 collective-permute-start.6
  18.6 0.0 collective-permute-done.refs_1_
  18.6 2.4 %collective-permute-done.7.refs_8_ = bf16[128,512]{1,0:T(8,128)(2,1)S(1)} collective-permute-done((bf16[128,512]{1,0:T(8,128)(2,1)S(1)}, bf16[128,512]{1,0:T(8,128)(2,1)S(1)}, u32[]{:S(2)}, u32[]{:S(2)}) %collective-permute-start.7) | collective-permute-done | bytes 131104 | tf_op jit(solution)/shard_map/ppermute | solution.py:427
  21.0 0.0 collective-permute-done.4.refs_5_
  21.0 0.0 collective-permute-done.2.refs_3_
  21.0 0.0 collective-permute-done.6.refs_7_
  21.1 1.9 %warp.1 = (bf16[8,16,640]{2,1,0:T(8,128)(2,1)S(1)}, bf16[128,512]{1,0:T(8,128)(2,1)S(1)}) custom-call(s32[1,1,1,4]{3,2,1,0:T(1,128)S(1)} %copy-done.5, s32[1,1,1,4]{3,2,1,0:T(1,128)S(1)} %copy-done.6, s32[1,1,1,4]{3,2,1,0:T(1,128)S(1)} %copy-done.7, s32[2,1,1,1,4]{4,3,2,1,0:T(1,128)S(1)} %copy-done.4, f32[1,1]{1,0:T(1,128)S(6)} %copy.13.blend, ...), custom_call_target="tpu_custom_call" | custom-call | tf_op jit(solution)/shard_map/warp/pallas_call | solution.py:156
  23.0 17.1 %all_to_all.10.got = bf16[8,16,640]{2,1,0:T(8,128)(2,1)S(1)} all-to-all(bf16[8,16,640]{2,1,0:T(8,128)(2,1)S(1)} %get-tuple-element.16), channel_id=1, replica_groups=mesh['gz'=8,'rows'=32] {'gz'}, dimensions={0} | all-to-all | bytes 327680 | tf_op jit(solution)/shard_map/all_to_all | solution.py:445
  40.1 0.8 %prior.1 = bf16[8,16,512]{2,1,0:T(8,128)(2,1)} custom-call(bf16[8,16,640]{2,1,0:T(8,128)(2,1)S(1)} %all_to_all.10.got), custom_call_target="tpu_custom_call" | custom-call | tf_op jit(solution)/shard_map/prior/pallas_call | solution.py:192
  40.9 3.5 %all-to-all-start.1 = ((bf16[8,16,512]{2,1,0:T(8,128)(2,1)}), bf16[8,16,512]{2,1,0:T(8,128)(2,1)S(1)}, u32[]{:S(2)}, u32[]{:S(2)}) async-start(bf16[8,16,512]{2,1,0:T(8,128)(2,1)} %prior.1), calls=%async_computation.1 | async-start | bytes 262144 | tf_op jit(solution)/shard_map/all_to_all | solution.py:447
  44.4 0.0 copy-start.2
  44.4 0.0 copy-start.3
  44.5 0.6 copy-done.2
  45.1 0.0 copy-done.3
  45.1 0.7 %weights.1 = (bf16[1024,256]{1,0:T(8,128)(2,1)S(1)}, bf16[288,256]{1,0:T(8,128)(2,1)S(1)}, bf16[2,576,256]{2,1,0:T(8,128)(2,1)S(1)}, f32[4,32,256]{2,1,0:T(8,128)S(1)}) custom-call(bf16[9,2,32]{2,1,0:T(2,128)(2,1)S(1)} %bitcast.12, bf16[9,32,32]{2,1,0:T(8,128)(2,1)S(1)} %copy-done.1, bf16[2,9,32,32]{3,2,1,0:T(8,128)(2,1)S(1)} %copy-done, ...), custom_call_target="tpu_custom_call" | custom-call | flops 20000000 | bytes 2000000 | tf_op jit(solution)/shard_map/weights/pallas_call | solution.py:71
  45.8 8.1 %all-to-all-done.1.prior = bf16[8,16,512]{2,1,0:T(8,128)(2,1)S(1)} async-done(((bf16[8,16,512]{2,1,0:T(8,128)(2,1)}), bf16[8,16,512]{2,1,0:T(8,128)(2,1)S(1)}, u32[]{:S(2)}, u32[]{:S(2)}) %all-to-all-start.1) | async-done | bytes 131104 | tf_op jit(solution)/shard_map/all_to_all | solution.py:447
  53.9 2.5 %collective-permute-start.9 = (bf16[2,16,512]{2,1,0:T(8,128)(2,1)S(1)}, bf16[2,16,512]{2,1,0:T(8,128)(2,1)S(1)}, u32[]{:S(2)}, u32[]{:S(2)}) collective-permute-start(bf16[2,16,512]{2,1,0:T(8,128)(2,1)S(1)} %pad_maximum_fusion), channel_id=1, source_target_pairs={{1,2},{2,1},{3,4},{4,3},{5,6},{6,5},{7,8},{8,7},{9,10},{10,9},{11,... | collective-permute-start | bytes 98312 | tf_op jit(solution)/shard_map/ppermute | solution.py:427
  56.5 0.2 collective-permute-start.8
  56.7 3.7 %middle.1 = (bf16[32,32,256]{2,1,0:T(8,128)(2,1)S(1)}, bf16[2,2,128,256]{3,2,1,0:T(8,128)(2,1)S(1)}, bf16[2,256,256]{2,1,0:T(8,128)(2,1)S(1)}, bf16[2,384,256]{2,1,0:T(8,128)(2,1)S(1)}) custom-call(bf16[128,512]{1,0:T(8,128)(2,1)S(1)} %get-tuple-element.15.enc, bf16[8,16,512]{2,1,0:T(8,128)(2,1)S(1)} %all-to-all-done.1.prior, ...), custom_call_target="tpu_custom_call" | custom-call | flops 6000000000 | bytes 4000000 | tf_op jit(solution)/shard_map/middle/pallas_call | solution.py:304
  60.3 0.0 collective-permute-done.9.outer
  60.4 0.0 collective-permute-done.8.inner
  60.4 2.8 %border.1 = bf16[1,1,32,64,256]{4,3,2,1,0:T(8,128)(2,1)} custom-call(bf16[128,512]{1,0:T(8,128)(2,1)S(1)} %get-tuple-element.15.enc, bf16[8,16,512]{2,1,0:T(8,128)(2,1)S(1)} %all-to-all-done.1.prior, bf16[2,16,512]{2,1,0:T(8,128)(2,1)S(1)} %collective-permute-done.8.inner, bf16[2,16,512]{2,1,0:T(8,128)(2,1)S(1)} %collective-permute-done.9.outer, ...), custom_call_target="tpu_custom_call" | custom-call | tf_op jit(solution)/shard_map/border/pallas_call | solution.py:391
  (20 shorter events, 0.0 us)
Async XLA Ops:
  0.0 21.0 %copy-start.6 = (s32[1,1,1,4]{3,2,1,0:T(1,128)S(1)}, s32[1,1,1,4]{3,2,1,0:T(1,128)}, u32[]{:S(2)}) copy-start(s32[1,1,1,4]{3,2,1,0:T(1,128)} %base.1) | copy-start | bytes 52
  0.0 21.1 %copy-start.7 = (s32[1,1,1,4]{3,2,1,0:T(1,128)S(1)}, s32[1,1,1,4]{3,2,1,0:T(1,128)}, u32[]{:S(2)}) copy-start(s32[1,1,1,4]{3,2,1,0:T(1,128)} %cols.1) | copy-start | bytes 52
  0.0 21.1 %copy-start.4 = (s32[2,1,1,1,4]{4,3,2,1,0:T(1,128)S(1)}, s32[2,1,1,1,4]{4,3,2,1,0:T(1,128)}, u32[]{:S(2)}) copy-start(s32[2,1,1,1,4]{4,3,2,1,0:T(1,128)} %frac.1) | copy-start | bytes 100
  0.0 21.1 %copy-start.5 = (s32[1,1,1,4]{3,2,1,0:T(1,128)S(1)}, s32[1,1,1,4]{3,2,1,0:T(1,128)}, u32[]{:S(2)}) copy-start(s32[1,1,1,4]{3,2,1,0:T(1,128)} %offs.1) | copy-start | bytes 52
  0.0 8.2 %collective-permute-start.1 = (bf16[128,512]{1,0:T(8,128)(2,1)}, bf16[128,512]{1,0:T(8,128)(2,1)S(1)}, u32[]{:S(2)}, u32[]{:S(2)}) collective-permute-start(bf16[128,512]{1,0:T(8,128)(2,1)} %bitcast.15), channel_id=1, source_target_pairs={{1,3},{2,0},{3,5},{4,2},{5,7},{6,4},{7,9},{8,6},{9,11},{10,8},{11,... | collective-permute-start | bytes 393224 | tf_op jit(solution)/shard_map/ppermute | solution.py:427
  3.4 12.0 %collective-permute-start.3 = (bf16[128,512]{1,0:T(8,128)(2,1)}, bf16[128,512]{1,0:T(8,128)(2,1)S(1)}, u32[]{:S(2)}, u32[]{:S(2)}) collective-permute-start(bf16[128,512]{1,0:T(8,128)(2,1)} %bitcast.16), channel_id=1, source_target_pairs={{0,2},{2,4},{3,1},{4,6},{5,3},{6,8},{7,5},{8,10},{9,7},{10,12},{11... | collective-permute-start | bytes 393224 | tf_op jit(solution)/shard_map/ppermute | solution.py:427
  8.2 9.7 %collective-permute-start.5 = (bf16[128,512]{1,0:T(8,128)(2,1)S(1)}, bf16[128,512]{1,0:T(8,128)(2,1)S(1)}, u32[]{:S(2)}, u32[]{:S(2)}) collective-permute-start(bf16[128,512]{1,0:T(8,128)(2,1)S(1)} %collective-permute-done.1.refs_2_), channel_id=1, source_target_pairs={{1,3},{2,0},{3,5},{4,2},{5,7},{6,4},{7,9},{8,6},{9,11},{10,8},{11,... | collective-permute-start | bytes 393224 | tf_op jit(solution)/shard_map/ppermute | solution.py:427
  10.1 8.5 %collective-permute-start = (bf16[128,512]{1,0:T(8,128)(2,1)}, bf16[128,512]{1,0:T(8,128)(2,1)S(1)}, u32[]{:S(2)}, u32[]{:S(2)}) collective-permute-start(bf16[128,512]{1,0:T(8,128)(2,1)} %bitcast.17), channel_id=1, source_target_pairs={{0,1},{1,0},{2,3},{3,2},{4,5},{5,4},{6,7},{7,6},{8,9},{9,8},{10,11... | collective-permute-start | bytes 393224 | tf_op jit(solution)/shard_map/ppermute | solution.py:427
  15.3 5.7 %collective-permute-start.7 = (bf16[128,512]{1,0:T(8,128)(2,1)S(1)}, bf16[128,512]{1,0:T(8,128)(2,1)S(1)}, u32[]{:S(2)}, u32[]{:S(2)}) collective-permute-start(bf16[128,512]{1,0:T(8,128)(2,1)S(1)} %collective-permute-done.3.refs_4_), channel_id=1, source_target_pairs={{3,1},{5,3},{7,5},{9,7},{11,9},{13,11},{15,13},{17,15},{19,17},{21... | collective-permute-start | bytes 393224 | tf_op jit(solution)/shard_map/ppermute | solution.py:427
  17.2 3.8 %collective-permute-start.4 = (bf16[128,512]{1,0:T(8,128)(2,1)S(1)}, bf16[128,512]{1,0:T(8,128)(2,1)S(1)}, u32[]{:S(2)}, u32[]{:S(2)}) collective-permute-start(bf16[128,512]{1,0:T(8,128)(2,1)S(1)} %collective-permute-done.3.refs_4_), channel_id=1, source_target_pairs={{0,1},{1,0},{2,3},{3,2},{4,5},{5,4},{6,7},{7,6},{8,9},{9,8},{10,11... | collective-permute-start | bytes 393224 | tf_op jit(solution)/shard_map/ppermute | solution.py:427
  17.3 3.7 %collective-permute-start.2 = (bf16[128,512]{1,0:T(8,128)(2,1)S(1)}, bf16[128,512]{1,0:T(8,128)(2,1)S(1)}, u32[]{:S(2)}, u32[]{:S(2)}) collective-permute-start(bf16[128,512]{1,0:T(8,128)(2,1)S(1)} %collective-permute-done.1.refs_2_), channel_id=1, source_target_pairs={{0,1},{1,0},{2,3},{3,2},{4,5},{5,4},{6,7},{7,6},{8,9},{9,8},{10,11... | collective-permute-start | bytes 393224 | tf_op jit(solution)/shard_map/ppermute | solution.py:427
  17.8 3.2 %collective-permute-start.6 = (bf16[128,512]{1,0:T(8,128)(2,1)S(1)}, bf16[128,512]{1,0:T(8,128)(2,1)S(1)}, u32[]{:S(2)}, u32[]{:S(2)}) collective-permute-start(bf16[128,512]{1,0:T(8,128)(2,1)S(1)} %collective-permute-done.5.refs_6_), channel_id=1, source_target_pairs={{0,1},{1,0},{2,3},{3,2},{4,5},{5,4},{6,7},{7,6},{8,9},{9,8},{10,11... | collective-permute-start | bytes 393224 | tf_op jit(solution)/shard_map/ppermute | solution.py:427
  40.9 3.6 %copy-start = (bf16[2,9,32,32]{3,2,1,0:T(8,128)(2,1)S(1)}, bf16[2,9,32,32]{3,2,1,0:T(8,128)(2,1)}, u32[]{:S(2)}) copy-start(bf16[2,9,32,32]{3,2,1,0:T(8,128)(2,1)} %kp.1) | copy-start | bytes 110596
  40.9 3.6 %copy-start.1 = (bf16[9,32,32]{2,1,0:T(8,128)(2,1)S(1)}, bf16[9,32,32]{2,1,0:T(8,128)(2,1)}, u32[]{:S(2)}) copy-start(bf16[9,32,32]{2,1,0:T(8,128)(2,1)} %kd.1) | copy-start | bytes 55300
  40.9 3.6 %copy-start.8 = (f32[32]{0:T(128)S(1)}, f32[32]{0:T(128)}, u32[]{:S(2)}) copy-start(f32[32]{0:T(128)} %param.19) | copy-start | bytes 388
  40.9 3.6 %copy-start.9 = (f32[32]{0:T(128)S(1)}, f32[32]{0:T(128)}, u32[]{:S(2)}) copy-start(f32[32]{0:T(128)} %param.21) | copy-start | bytes 388
  40.9 13.0 %all-to-all-start.1 = ((bf16[8,16,512]{2,1,0:T(8,128)(2,1)}), bf16[8,16,512]{2,1,0:T(8,128)(2,1)S(1)}, u32[]{:S(2)}, u32[]{:S(2)}) async-start(bf16[8,16,512]{2,1,0:T(8,128)(2,1)} %prior.1), calls=%async_computation.1 | async-start | bytes 262144 | tf_op jit(solution)/shard_map/all_to_all | solution.py:447
  44.4 0.7 %copy-start.2 = (bf16[9,32,2]{1,2,0:T(2,128)(2,1)S(1)}, bf16[9,32,2]{1,2,0:T(2,128)(2,1)}, u32[]{:S(2)}) copy-start(bf16[9,32,2]{1,2,0:T(2,128)(2,1)} %param.18) | copy-start | bytes 3460
  44.4 0.7 %copy-start.3 = (f32[2,32]{1,0:T(2,128)S(1)}, f32[2,32]{1,0:T(2,128)}, u32[]{:S(2)}) copy-start(f32[2,32]{1,0:T(2,128)} %bp.1) | copy-start | bytes 772
  53.9 6.4 %collective-permute-start.9 = (bf16[2,16,512]{2,1,0:T(8,128)(2,1)S(1)}, bf16[2,16,512]{2,1,0:T(8,128)(2,1)S(1)}, u32[]{:S(2)}, u32[]{:S(2)}) collective-permute-start(bf16[2,16,512]{2,1,0:T(8,128)(2,1)S(1)} %pad_maximum_fusion), channel_id=1, source_target_pairs={{1,2},{2,1},{3,4},{4,3},{5,6},{6,5},{7,8},{8,7},{9,10},{10,9},{11,... | collective-permute-start | bytes 98312 | tf_op jit(solution)/shard_map/ppermute | solution.py:427
  56.5 3.9 %collective-permute-start.8 = (bf16[2,16,512]{2,1,0:T(8,128)(2,1)S(1)}, bf16[2,16,512]{2,1,0:T(8,128)(2,1)S(1)}, u32[]{:S(2)}, u32[]{:S(2)}) collective-permute-start(bf16[2,16,512]{2,1,0:T(8,128)(2,1)S(1)} %pad_maximum_fusion), channel_id=1, source_target_pairs={{0,1},{1,0},{2,3},{3,2},{4,5},{5,4},{6,7},{7,6},{8,9},{9,8},{10,11... | collective-permute-start | bytes 98312 | tf_op jit(solution)/shard_map/ppermute | solution.py:427

commit v4 on v3

--- a/solution.py
+++ b/solution.py
@@ -87,15 +87,31 @@
 OFFSETS = (0, 1, 2, -1, -2, 3, 4, -3, -4)
 
 
+def hold_kernel(own, held, sem):
+    fetch = pltpu.make_async_copy(own, held, sem)
+    fetch.start()
+    fetch.wait()
+
+
+def make_hold(own):
+    own = pltpu.with_memory_space_constraint(own, pltpu.HBM)
+    return pl.pallas_call(
+        hold_kernel,
+        out_shape=jax.ShapeDtypeStruct((128, 512), BF16),
+        in_specs=[pl.BlockSpec(memory_space=pltpu.HBM)],
+        out_specs=vspec(),
+        scratch_shapes=[pltpu.SemaphoreType.DMA],
+        compiler_params=pltpu.CompilerParams(vmem_limit_bytes=4 << 20),
+        name="hold",
+    )(own)
+
+
 def warp_kernel(offs, base, cols, frac, blend, *refs):
-    blocks, (pay, enc, S, MJ, MV, sem) = refs[:9], refs[9:]
+    blocks, (pay, enc, S, MJ, MV) = refs[:9], refs[9:]
     core = lax.rem(lax.axis_index("rows"), 2)
     sign = 1 - 2 * core
-    fetch = pltpu.make_async_copy(blocks[0], S.at[4], sem)
-    fetch.start()
     for k, off in enumerate(OFFSETS):
-        if k > 0:
-            S[4 + sign * off] = blocks[k][...]
+        S[4 + sign * off] = blocks[k][...]
     mats = []
     for j in range(4):
         lo, hi = max(j - 1, 0), min(j + 1, 3)
@@ -110,7 +126,6 @@
         target = cols[0, 0, 0, j] + x
         mat = jnp.where(src == target, 1.0 - q, 0.0) + jnp.where(src == target + 1, q, 0.0)
         mats.append(mat.astype(BF16))
-    fetch.wait()
     for j in range(4):
         lo, hi = max(j - 1, 0), min(j + 1, 3)
         first = offs[0, 0, 0, j] + 4
@@ -152,24 +167,22 @@
 
 
 def make_warp(offs, base, cols, frac, blend, blocks):
-    own = pltpu.with_memory_space_constraint(blocks[0], pltpu.HBM)
     return pl.pallas_call(
         warp_kernel,
         out_shape=(
             jax.ShapeDtypeStruct((8, 16, 640), BF16),
             jax.ShapeDtypeStruct((128, 512), BF16),
         ),
-        in_specs=[sspec()] * 5 + [pl.BlockSpec(memory_space=pltpu.HBM)] + [vspec()] * 8,
+        in_specs=[sspec()] * 5 + [vspec()] * 9,
         out_specs=(vspec(), vspec()),
         scratch_shapes=[
             VMEM((9, 128, 512), BF16),
             VMEM((4, 264, 128), F32),
             VMEM((136, 512), F32),
-            pltpu.SemaphoreType.DMA,
         ],
         compiler_params=pltpu.CompilerParams(vmem_limit_bytes=8 << 20),
         name="warp",
-    )(offs, base, cols, frac, blend, own, *blocks[1:])
+    )(offs, base, cols, frac, blend, *blocks)
 
 
 def prior_kernel(got, out, M):
@@ -438,9 +451,10 @@
     w1, wd, wp, bb = make_weights(
         conv_first, conv_down, conv_deep, bias_first, bias_down, bias_deep
     )
+    held = make_hold(own)
     pay, enc = make_warp(
         block_offset, row_base, col_base, fractions, blend,
-        (own, a, p1, sp1, p2, sp2, f1, sf1, f2),
+        (held, a, p1, sp1, p2, sp2, f1, sf1, f2),
     )
     got = lax.all_to_all(pay, "gz", 0, 0)
     given = make_prior(got)

time: 64.2 us -> 64.1 us (level)
  waiting for transfers between devices: 11.2 us -> 8.86 us
  starting transfers between devices: 23.5 us -> 24.8 us
  blocking collectives: 17.1 us -> 17.9 us
    all_to_all x1, waiting for transfers between devices: 8.11 us -> 6.78 us  [per_device(): prior = lax.all_to_all(given, 'gz', 0, 0)]
    ppermute x10, starting transfers between devices: 20 us -> 21.3 us  [send(): return lax.ppermute(value, 'rows', route)]
    ppermute x10, waiting for transfers between devices: 3.07 us -> 2.08 us  [send(): return lax.ppermute(value, 'rows', route)]
    pallas_call x0 -> x1, Pallas kernels: none -> 0.94 us  [make_hold(): pl.pallas_call(hold_kernel, out_shape=jax.ShapeDtypeStruct((128, 512), BF...]
    all_to_all x1, blocking collectives: 17.1 us -> 17.9 us  [per_device(): got = lax.all_to_all(pay, 'gz', 0, 0)]
    pallas_call x1, Pallas kernels: 1.94 us -> 1.11 us  [make_warp(): pl.pallas_call(warp_kernel, out_shape=(jax.ShapeDtypeStruct((8, 16, 640),...]
  transfers between devices with their start and end apart: 11 -> 11, of which waited for: 3 -> 3; matrix products, arithmetic and copies ran while one was open for 0% -> 0% of each run, Pallas kernels for 7% -> 8%
where the time goes in v4:
time: 64.1 us; the launch traced here: 63.2 us
  starting transfers between devices  24.8 us (39%)
  blocking collectives  17.9 us (28%)
  Pallas kernels  9.97 us (16%)
  waiting for transfers between devices  8.86 us (14%)
  between operations  0.89 us (1%)
  local copies, waits for them, and re-layouts  0.68 us (1%)
    ppermute x10, starting transfers between devices, send(): return lax.ppermute(value, 'rows', route)  21.3 us
    all_to_all x1, blocking collectives, per_device(): got = lax.all_to_all(pay, 'gz', 0, 0)  17.9 us
    all_to_all x1, waiting for transfers between devices, per_device(): prior = lax.all_to_all(given, 'gz', 0, 0)  6.78 us
    pallas_call x1, Pallas kernels, make_inner(): pl.pallas_call(inner_kernel, out_shape=(jax.ShapeDtypeStruct((32, 32, 256...  3.67 us
    all_to_all x1, starting transfers between devices, per_device(): prior = lax.all_to_all(given, 'gz', 0, 0)  3.52 us
    pallas_call x1, Pallas kernels, make_outer(): pl.pallas_call(outer_kernel, out_shape=jax.ShapeDtypeStruct((1, 1, 32, 64...  2.82 us
    ppermute x10, waiting for transfers between devices, send(): return lax.ppermute(value, 'rows', route)  2.08 us
  transfers between devices with their start and end apart: 11, of which 3 were waited for; matrix products, arithmetic and copies ran while one was open for 0% of the time, Pallas kernels for 8%

profile of v4, /device:TPU:7, one launch (start us, length us, event | category | flops | bytes accessed | tf_op | source)
XLA Modules:
  0.0 63.2 jit_solution(13127459066500228454)
XLA Ops:
  0.0 3.2 %collective-permute-start.1 = (bf16[128,512]{1,0:T(8,128)(2,1)}, bf16[128,512]{1,0:T(8,128)(2,1)S(1)}, u32[]{:S(2)}, u32[]{:S(2)}) collective-permute-start(bf16[128,512]{1,0:T(8,128)(2,1)} %bitcast.15), channel_id=1, source_target_pairs={{1,3},{2,0},{3,5},{4,2},{5,7},{6,4},{7,9},{8,6},{9,11},{10,8},{11,... | collective-permute-start | bytes 393224 | tf_op jit(solution)/shard_map/ppermute | solution.py:440
  3.2 4.2 %collective-permute-start.3 = (bf16[128,512]{1,0:T(8,128)(2,1)}, bf16[128,512]{1,0:T(8,128)(2,1)S(1)}, u32[]{:S(2)}, u32[]{:S(2)}) collective-permute-start(bf16[128,512]{1,0:T(8,128)(2,1)} %bitcast.16), channel_id=1, source_target_pairs={{0,2},{2,4},{3,1},{4,6},{5,3},{6,8},{7,5},{8,10},{9,7},{10,12},{11... | collective-permute-start | bytes 393224 | tf_op jit(solution)/shard_map/ppermute | solution.py:440
  7.4 0.6 collective-permute-done.1.refs_2_
  8.0 1.9 %collective-permute-start.5 = (bf16[128,512]{1,0:T(8,128)(2,1)S(1)}, bf16[128,512]{1,0:T(8,128)(2,1)S(1)}, u32[]{:S(2)}, u32[]{:S(2)}) collective-permute-start(bf16[128,512]{1,0:T(8,128)(2,1)S(1)} %collective-permute-done.1.refs_2_), channel_id=1, source_target_pairs={{1,3},{2,0},{3,5},{4,2},{5,7},{6,4},{7,9},{8,6},{9,11},{10,8},{11,... | collective-permute-start | bytes 393224 | tf_op jit(solution)/shard_map/ppermute | solution.py:440
  9.9 5.2 %collective-permute-start = (bf16[128,512]{1,0:T(8,128)(2,1)}, bf16[128,512]{1,0:T(8,128)(2,1)S(1)}, u32[]{:S(2)}, u32[]{:S(2)}) collective-permute-start(bf16[128,512]{1,0:T(8,128)(2,1)} %bitcast.17), channel_id=1, source_target_pairs={{0,1},{1,0},{2,3},{3,2},{4,5},{5,4},{6,7},{7,6},{8,9},{9,8},{10,11... | collective-permute-start | bytes 393224 | tf_op jit(solution)/shard_map/ppermute | solution.py:440
  15.2 0.0 collective-permute-done.3.refs_4_
  15.2 1.9 %collective-permute-start.7 = (bf16[128,512]{1,0:T(8,128)(2,1)S(1)}, bf16[128,512]{1,0:T(8,128)(2,1)S(1)}, u32[]{:S(2)}, u32[]{:S(2)}) collective-permute-start(bf16[128,512]{1,0:T(8,128)(2,1)S(1)} %collective-permute-done.3.refs_4_), channel_id=1, source_target_pairs={{3,1},{5,3},{7,5},{9,7},{11,9},{13,11},{15,13},{17,15},{19,17},{21... | collective-permute-start | bytes 393224 | tf_op jit(solution)/shard_map/ppermute | solution.py:440
  17.1 0.1 collective-permute-start.4
  17.2 0.5 collective-permute-start.2
  17.7 0.1 collective-permute-start.6
  17.8 0.9 %hold.1.refs_0_ = bf16[128,512]{1,0:T(8,128)(2,1)S(1)} custom-call(bf16[128,512]{1,0:T(8,128)(2,1)} %bitcast.18), custom_call_target="tpu_custom_call" | custom-call | tf_op jit(solution)/shard_map/hold/pallas_call | solution.py:98
  18.7 0.0 copy-start.4
  18.7 0.0 copy-start.5
  19.4 1.4 %collective-permute-done.7.refs_8_ = bf16[128,512]{1,0:T(8,128)(2,1)S(1)} collective-permute-done((bf16[128,512]{1,0:T(8,128)(2,1)S(1)}, bf16[128,512]{1,0:T(8,128)(2,1)S(1)}, u32[]{:S(2)}, u32[]{:S(2)}) %collective-permute-start.7) | collective-permute-done | bytes 131104 | tf_op jit(solution)/shard_map/ppermute | solution.py:440
  20.9 0.0 collective-permute-done.4.refs_5_
  20.9 0.0 collective-permute-done.2.refs_3_
  20.9 0.0 collective-permute-done.6.refs_7_
  20.9 1.1 %warp.1 = (bf16[8,16,640]{2,1,0:T(8,128)(2,1)S(1)}, bf16[128,512]{1,0:T(8,128)(2,1)S(1)}) custom-call(s32[1,1,1,4]{3,2,1,0:T(1,128)S(1)} %copy-done.5, s32[1,1,1,4]{3,2,1,0:T(1,128)S(1)} %copy-done.6, s32[1,1,1,4]{3,2,1,0:T(1,128)S(1)} %copy-done.7, s32[2,1,1,1,4]{4,3,2,1,0:T(1,128)S(1)} %copy-done.4, f32[1,1]{1,0:T(1,128)S(6)} %copy.13.blend, ...), custom_call_target="tpu_custom_call" | custom-call | tf_op jit(solution)/shard_map/warp/pallas_call | solution.py:170
  22.0 17.9 %all_to_all.10.got = bf16[8,16,640]{2,1,0:T(8,128)(2,1)S(1)} all-to-all(bf16[8,16,640]{2,1,0:T(8,128)(2,1)S(1)} %get-tuple-element.16), channel_id=1, replica_groups=mesh['gz'=8,'rows'=32] {'gz'}, dimensions={0} | all-to-all | bytes 327680 | tf_op jit(solution)/shard_map/all_to_all | solution.py:459
  40.0 0.8 %prior.1 = bf16[8,16,512]{2,1,0:T(8,128)(2,1)} custom-call(bf16[8,16,640]{2,1,0:T(8,128)(2,1)S(1)} %all_to_all.10.got), custom_call_target="tpu_custom_call" | custom-call | tf_op jit(solution)/shard_map/prior/pallas_call | solution.py:205
  40.7 3.5 %all-to-all-start.1 = ((bf16[8,16,512]{2,1,0:T(8,128)(2,1)}), bf16[8,16,512]{2,1,0:T(8,128)(2,1)S(1)}, u32[]{:S(2)}, u32[]{:S(2)}) async-start(bf16[8,16,512]{2,1,0:T(8,128)(2,1)} %prior.1), calls=%async_computation.1 | async-start | bytes 262144 | tf_op jit(solution)/shard_map/all_to_all | solution.py:461
  44.3 0.0 copy-start.2
  44.3 0.0 copy-start.3
  44.3 0.6 copy-done.2
  45.0 0.0 copy-done.3
  45.0 0.7 %weights.1 = (bf16[1024,256]{1,0:T(8,128)(2,1)S(1)}, bf16[288,256]{1,0:T(8,128)(2,1)S(1)}, bf16[2,576,256]{2,1,0:T(8,128)(2,1)S(1)}, f32[4,32,256]{2,1,0:T(8,128)S(1)}) custom-call(bf16[9,2,32]{2,1,0:T(2,128)(2,1)S(1)} %bitcast.12, bf16[9,32,32]{2,1,0:T(8,128)(2,1)S(1)} %copy-done.1, bf16[2,9,32,32]{3,2,1,0:T(8,128)(2,1)S(1)} %copy-done, ...), custom_call_target="tpu_custom_call" | custom-call | flops 20000000 | bytes 2000000 | tf_op jit(solution)/shard_map/weights/pallas_call | solution.py:71
  45.6 6.8 %all-to-all-done.1.prior = bf16[8,16,512]{2,1,0:T(8,128)(2,1)S(1)} async-done(((bf16[8,16,512]{2,1,0:T(8,128)(2,1)}), bf16[8,16,512]{2,1,0:T(8,128)(2,1)S(1)}, u32[]{:S(2)}, u32[]{:S(2)}) %all-to-all-start.1) | async-done | bytes 131104 | tf_op jit(solution)/shard_map/all_to_all | solution.py:461
  52.4 3.5 %collective-permute-start.9 = (bf16[2,16,512]{2,1,0:T(8,128)(2,1)S(1)}, bf16[2,16,512]{2,1,0:T(8,128)(2,1)S(1)}, u32[]{:S(2)}, u32[]{:S(2)}) collective-permute-start(bf16[2,16,512]{2,1,0:T(8,128)(2,1)S(1)} %pad_maximum_fusion), channel_id=1, source_target_pairs={{1,2},{2,1},{3,4},{4,3},{5,6},{6,5},{7,8},{8,7},{9,10},{10,9},{11,... | collective-permute-start | bytes 98312 | tf_op jit(solution)/shard_map/ppermute | solution.py:440
  55.9 0.7 %collective-permute-start.8 = (bf16[2,16,512]{2,1,0:T(8,128)(2,1)S(1)}, bf16[2,16,512]{2,1,0:T(8,128)(2,1)S(1)}, u32[]{:S(2)}, u32[]{:S(2)}) collective-permute-start(bf16[2,16,512]{2,1,0:T(8,128)(2,1)S(1)} %pad_maximum_fusion), channel_id=1, source_target_pairs={{0,1},{1,0},{2,3},{3,2},{4,5},{5,4},{6,7},{7,6},{8,9},{9,8},{10,11... | collective-permute-start | bytes 98312 | tf_op jit(solution)/shard_map/ppermute | solution.py:440
  56.6 3.7 %middle.1 = (bf16[32,32,256]{2,1,0:T(8,128)(2,1)S(1)}, bf16[2,2,128,256]{3,2,1,0:T(8,128)(2,1)S(1)}, bf16[2,256,256]{2,1,0:T(8,128)(2,1)S(1)}, bf16[2,384,256]{2,1,0:T(8,128)(2,1)S(1)}) custom-call(bf16[128,512]{1,0:T(8,128)(2,1)S(1)} %get-tuple-element.15.enc, bf16[8,16,512]{2,1,0:T(8,128)(2,1)S(1)} %all-to-all-done.1.prior, ...), custom_call_target="tpu_custom_call" | custom-call | flops 6000000000 | bytes 4000000 | tf_op jit(solution)/shard_map/middle/pallas_call | solution.py:317
  60.3 0.0 collective-permute-done.9.outer
  60.3 2.8 %border.1 = bf16[1,1,32,64,256]{4,3,2,1,0:T(8,128)(2,1)} custom-call(bf16[128,512]{1,0:T(8,128)(2,1)S(1)} %get-tuple-element.15.enc, bf16[8,16,512]{2,1,0:T(8,128)(2,1)S(1)} %all-to-all-done.1.prior, bf16[2,16,512]{2,1,0:T(8,128)(2,1)S(1)} %collective-permute-done.8.inner, bf16[2,16,512]{2,1,0:T(8,128)(2,1)S(1)} %collective-permute-done.9.outer, ...), custom_call_target="tpu_custom_call" | custom-call | tf_op jit(solution)/shard_map/border/pallas_call | solution.py:404
  (21 shorter events, 0.1 us)
Async XLA Ops:
  0.0 8.0 %collective-permute-start.1 = (bf16[128,512]{1,0:T(8,128)(2,1)}, bf16[128,512]{1,0:T(8,128)(2,1)S(1)}, u32[]{:S(2)}, u32[]{:S(2)}) collective-permute-start(bf16[128,512]{1,0:T(8,128)(2,1)} %bitcast.15), channel_id=1, source_target_pairs={{1,3},{2,0},{3,5},{4,2},{5,7},{6,4},{7,9},{8,6},{9,11},{10,8},{11,... | collective-permute-start | bytes 393224 | tf_op jit(solution)/shard_map/ppermute | solution.py:440
  3.2 12.0 %collective-permute-start.3 = (bf16[128,512]{1,0:T(8,128)(2,1)}, bf16[128,512]{1,0:T(8,128)(2,1)S(1)}, u32[]{:S(2)}, u32[]{:S(2)}) collective-permute-start(bf16[128,512]{1,0:T(8,128)(2,1)} %bitcast.16), channel_id=1, source_target_pairs={{0,2},{2,4},{3,1},{4,6},{5,3},{6,8},{7,5},{8,10},{9,7},{10,12},{11... | collective-permute-start | bytes 393224 | tf_op jit(solution)/shard_map/ppermute | solution.py:440
  8.0 9.7 %collective-permute-start.5 = (bf16[128,512]{1,0:T(8,128)(2,1)S(1)}, bf16[128,512]{1,0:T(8,128)(2,1)S(1)}, u32[]{:S(2)}, u32[]{:S(2)}) collective-permute-start(bf16[128,512]{1,0:T(8,128)(2,1)S(1)} %collective-permute-done.1.refs_2_), channel_id=1, source_target_pairs={{1,3},{2,0},{3,5},{4,2},{5,7},{6,4},{7,9},{8,6},{9,11},{10,8},{11,... | collective-permute-start | bytes 393224 | tf_op jit(solution)/shard_map/ppermute | solution.py:440
  9.9 9.5 %collective-permute-start = (bf16[128,512]{1,0:T(8,128)(2,1)}, bf16[128,512]{1,0:T(8,128)(2,1)S(1)}, u32[]{:S(2)}, u32[]{:S(2)}) collective-permute-start(bf16[128,512]{1,0:T(8,128)(2,1)} %bitcast.17), channel_id=1, source_target_pairs={{0,1},{1,0},{2,3},{3,2},{4,5},{5,4},{6,7},{7,6},{8,9},{9,8},{10,11... | collective-permute-start | bytes 393224 | tf_op jit(solution)/shard_map/ppermute | solution.py:440
  15.2 5.7 %collective-permute-start.7 = (bf16[128,512]{1,0:T(8,128)(2,1)S(1)}, bf16[128,512]{1,0:T(8,128)(2,1)S(1)}, u32[]{:S(2)}, u32[]{:S(2)}) collective-permute-start(bf16[128,512]{1,0:T(8,128)(2,1)S(1)} %collective-permute-done.3.refs_4_), channel_id=1, source_target_pairs={{3,1},{5,3},{7,5},{9,7},{11,9},{13,11},{15,13},{17,15},{19,17},{21... | collective-permute-start | bytes 393224 | tf_op jit(solution)/shard_map/ppermute | solution.py:440
  17.1 3.8 %collective-permute-start.4 = (bf16[128,512]{1,0:T(8,128)(2,1)S(1)}, bf16[128,512]{1,0:T(8,128)(2,1)S(1)}, u32[]{:S(2)}, u32[]{:S(2)}) collective-permute-start(bf16[128,512]{1,0:T(8,128)(2,1)S(1)} %collective-permute-done.3.refs_4_), channel_id=1, source_target_pairs={{0,1},{1,0},{2,3},{3,2},{4,5},{5,4},{6,7},{7,6},{8,9},{9,8},{10,11... | collective-permute-start | bytes 393224 | tf_op jit(solution)/shard_map/ppermute | solution.py:440
  17.2 3.7 %collective-permute-start.2 = (bf16[128,512]{1,0:T(8,128)(2,1)S(1)}, bf16[128,512]{1,0:T(8,128)(2,1)S(1)}, u32[]{:S(2)}, u32[]{:S(2)}) collective-permute-start(bf16[128,512]{1,0:T(8,128)(2,1)S(1)} %collective-permute-done.1.refs_2_), channel_id=1, source_target_pairs={{0,1},{1,0},{2,3},{3,2},{4,5},{5,4},{6,7},{7,6},{8,9},{9,8},{10,11... | collective-permute-start | bytes 393224 | tf_op jit(solution)/shard_map/ppermute | solution.py:440
  17.7 3.2 %collective-permute-start.6 = (bf16[128,512]{1,0:T(8,128)(2,1)S(1)}, bf16[128,512]{1,0:T(8,128)(2,1)S(1)}, u32[]{:S(2)}, u32[]{:S(2)}) collective-permute-start(bf16[128,512]{1,0:T(8,128)(2,1)S(1)} %collective-permute-done.5.refs_6_), channel_id=1, source_target_pairs={{0,1},{1,0},{2,3},{3,2},{4,5},{5,4},{6,7},{7,6},{8,9},{9,8},{10,11... | collective-permute-start | bytes 393224 | tf_op jit(solution)/shard_map/ppermute | solution.py:440
  17.8 3.1 %copy-start.6 = (s32[1,1,1,4]{3,2,1,0:T(1,128)S(1)}, s32[1,1,1,4]{3,2,1,0:T(1,128)}, u32[]{:S(2)}) copy-start(s32[1,1,1,4]{3,2,1,0:T(1,128)} %base.1) | copy-start | bytes 52
  17.8 3.1 %copy-start.7 = (s32[1,1,1,4]{3,2,1,0:T(1,128)S(1)}, s32[1,1,1,4]{3,2,1,0:T(1,128)}, u32[]{:S(2)}) copy-start(s32[1,1,1,4]{3,2,1,0:T(1,128)} %cols.1) | copy-start | bytes 52
  18.7 2.2 %copy-start.4 = (s32[2,1,1,1,4]{4,3,2,1,0:T(1,128)S(1)}, s32[2,1,1,1,4]{4,3,2,1,0:T(1,128)}, u32[]{:S(2)}) copy-start(s32[2,1,1,1,4]{4,3,2,1,0:T(1,128)} %frac.1) | copy-start | bytes 100
  18.7 2.2 %copy-start.5 = (s32[1,1,1,4]{3,2,1,0:T(1,128)S(1)}, s32[1,1,1,4]{3,2,1,0:T(1,128)}, u32[]{:S(2)}) copy-start(s32[1,1,1,4]{3,2,1,0:T(1,128)} %offs.1) | copy-start | bytes 52
  40.7 3.6 %copy-start = (bf16[2,9,32,32]{3,2,1,0:T(8,128)(2,1)S(1)}, bf16[2,9,32,32]{3,2,1,0:T(8,128)(2,1)}, u32[]{:S(2)}) copy-start(bf16[2,9,32,32]{3,2,1,0:T(8,128)(2,1)} %kp.1) | copy-start | bytes 110596
  40.7 3.6 %copy-start.1 = (bf16[9,32,32]{2,1,0:T(8,128)(2,1)S(1)}, bf16[9,32,32]{2,1,0:T(8,128)(2,1)}, u32[]{:S(2)}) copy-start(bf16[9,32,32]{2,1,0:T(8,128)(2,1)} %kd.1) | copy-start | bytes 55300
  40.7 3.6 %copy-start.8 = (f32[32]{0:T(128)S(1)}, f32[32]{0:T(128)}, u32[]{:S(2)}) copy-start(f32[32]{0:T(128)} %param.19) | copy-start | bytes 388
  40.7 3.6 %copy-start.9 = (f32[32]{0:T(128)S(1)}, f32[32]{0:T(128)}, u32[]{:S(2)}) copy-start(f32[32]{0:T(128)} %param.21) | copy-start | bytes 388
  40.7 11.7 %all-to-all-start.1 = ((bf16[8,16,512]{2,1,0:T(8,128)(2,1)}), bf16[8,16,512]{2,1,0:T(8,128)(2,1)S(1)}, u32[]{:S(2)}, u32[]{:S(2)}) async-start(bf16[8,16,512]{2,1,0:T(8,128)(2,1)} %prior.1), calls=%async_computation.1 | async-start | bytes 262144 | tf_op jit(solution)/shard_map/all_to_all | solution.py:461
  44.3 0.7 %copy-start.2 = (bf16[9,32,2]{1,2,0:T(2,128)(2,1)S(1)}, bf16[9,32,2]{1,2,0:T(2,128)(2,1)}, u32[]{:S(2)}) copy-start(bf16[9,32,2]{1,2,0:T(2,128)(2,1)} %param.18) | copy-start | bytes 3460
  44.3 0.7 %copy-start.3 = (f32[2,32]{1,0:T(2,128)S(1)}, f32[2,32]{1,0:T(2,128)}, u32[]{:S(2)}) copy-start(f32[2,32]{1,0:T(2,128)} %bp.1) | copy-start | bytes 772
  52.4 7.9 %collective-permute-start.9 = (bf16[2,16,512]{2,1,0:T(8,128)(2,1)S(1)}, bf16[2,16,512]{2,1,0:T(8,128)(2,1)S(1)}, u32[]{:S(2)}, u32[]{:S(2)}) collective-permute-start(bf16[2,16,512]{2,1,0:T(8,128)(2,1)S(1)} %pad_maximum_fusion), channel_id=1, source_target_pairs={{1,2},{2,1},{3,4},{4,3},{5,6},{6,5},{7,8},{8,7},{9,10},{10,9},{11,... | collective-permute-start | bytes 98312 | tf_op jit(solution)/shard_map/ppermute | solution.py:440
  55.9 4.4 %collective-permute-start.8 = (bf16[2,16,512]{2,1,0:T(8,128)(2,1)S(1)}, bf16[2,16,512]{2,1,0:T(8,128)(2,1)S(1)}, u32[]{:S(2)}, u32[]{:S(2)}) collective-permute-start(bf16[2,16,512]{2,1,0:T(8,128)(2,1)S(1)} %pad_maximum_fusion), channel_id=1, source_target_pairs={{0,1},{1,0},{2,3},{3,2},{4,5},{5,4},{6,7},{7,6},{8,9},{9,8},{10,11... | collective-permute-start | bytes 98312 | tf_op jit(solution)/shard_map/ppermute | solution.py:440

commit v5 on v4

--- a/solution.py
+++ b/solution.py
@@ -185,10 +185,12 @@
     )(offs, base, cols, frac, blend, *blocks)
 
 
-def prior_kernel(got, out, M):
+def prior_kernel(got, given, M, out, sems):
+    copies = [pltpu.make_async_copy(out.at[s], given.at[s], sems.at[s]) for s in range(8)]
     state = jnp.zeros((16, 512), F32)
     for s in range(8):
         out[s] = state.astype(BF16)
+        copies[s].start()
         if s == 7:
             break
         M[s, 0:16, :] = got[s, :, 0:512].astype(F32)
@@ -199,6 +201,8 @@
         rate = extra[8:9, 0:1] + extra[9:10, 0:1] + extra[10:11, 0:1]
         warped = (1.0 - p) * M[s, 0:16, :] + p * M[s, 1:17, :]
         state = rate * state + (1.0 - rate) * warped
+    for copy in copies:
+        copy.wait()
 
 
 def make_prior(got):
@@ -206,8 +210,8 @@
         prior_kernel,
         out_shape=jax.ShapeDtypeStruct((8, 16, 512), BF16),
         in_specs=[vspec()],
-        out_specs=vspec(),
-        scratch_shapes=[VMEM((7, 24, 512), F32)],
+        out_specs=pl.BlockSpec(memory_space=pltpu.HBM),
+        scratch_shapes=[VMEM((7, 24, 512), F32), VMEM((8, 16, 512), BF16), pltpu.SemaphoreType.DMA((8,))],
         compiler_params=pltpu.CompilerParams(vmem_limit_bytes=4 << 20),
         name="prior",
     )(got)

time: 64.1 us -> 64.2 us (level)
  no operation moved by 1% of the time
where the time goes in v5:
time: 64.2 us; the launch traced here: 63.2 us
  starting transfers between devices  24.8 us (39%)
  blocking collectives  17.9 us (28%)
  Pallas kernels  9.98 us (16%)
  waiting for transfers between devices  8.85 us (14%)
  between operations  0.93 us (1%)
  local copies, waits for them, and re-layouts  0.69 us (1%)
    ppermute x10, starting transfers between devices, send(): return lax.ppermute(value, 'rows', route)  21.3 us
    all_to_all x1, blocking collectives, per_device(): got = lax.all_to_all(pay, 'gz', 0, 0)  17.9 us
    all_to_all x1, waiting for transfers between devices, per_device(): prior = lax.all_to_all(given, 'gz', 0, 0)  6.78 us
    pallas_call x1, Pallas kernels, make_inner(): pl.pallas_call(inner_kernel, out_shape=(jax.ShapeDtypeStruct((32, 32, 256...  3.67 us
    all_to_all x1, starting transfers between devices, per_device(): prior = lax.all_to_all(given, 'gz', 0, 0)  3.52 us
    pallas_call x1, Pallas kernels, make_outer(): pl.pallas_call(outer_kernel, out_shape=jax.ShapeDtypeStruct((1, 1, 32, 64...  2.82 us
    ppermute x10, waiting for transfers between devices, send(): return lax.ppermute(value, 'rows', route)  2.08 us
  transfers between devices with their start and end apart: 11, of which 3 were waited for; matrix products, arithmetic and copies ran while one was open for 0% of the time, Pallas kernels for 8%

profile of v5, /device:TPU:7, one launch (start us, length us, event | category | flops | bytes accessed | tf_op | source)
XLA Modules:
  0.0 63.2 jit_solution(13761510269893286035)
XLA Ops:
  0.0 3.2 %collective-permute-start.1 = (bf16[128,512]{1,0:T(8,128)(2,1)}, bf16[128,512]{1,0:T(8,128)(2,1)S(1)}, u32[]{:S(2)}, u32[]{:S(2)}) collective-permute-start(bf16[128,512]{1,0:T(8,128)(2,1)} %bitcast.15), channel_id=1, source_target_pairs={{1,3},{2,0},{3,5},{4,2},{5,7},{6,4},{7,9},{8,6},{9,11},{10,8},{11,... | collective-permute-start | bytes 393224 | tf_op jit(solution)/shard_map/ppermute | solution.py:444
  3.2 4.2 %collective-permute-start.3 = (bf16[128,512]{1,0:T(8,128)(2,1)}, bf16[128,512]{1,0:T(8,128)(2,1)S(1)}, u32[]{:S(2)}, u32[]{:S(2)}) collective-permute-start(bf16[128,512]{1,0:T(8,128)(2,1)} %bitcast.16), channel_id=1, source_target_pairs={{0,2},{2,4},{3,1},{4,6},{5,3},{6,8},{7,5},{8,10},{9,7},{10,12},{11... | collective-permute-start | bytes 393224 | tf_op jit(solution)/shard_map/ppermute | solution.py:444
  7.4 0.6 collective-permute-done.1.refs_2_
  8.0 1.9 %collective-permute-start.5 = (bf16[128,512]{1,0:T(8,128)(2,1)S(1)}, bf16[128,512]{1,0:T(8,128)(2,1)S(1)}, u32[]{:S(2)}, u32[]{:S(2)}) collective-permute-start(bf16[128,512]{1,0:T(8,128)(2,1)S(1)} %collective-permute-done.1.refs_2_), channel_id=1, source_target_pairs={{1,3},{2,0},{3,5},{4,2},{5,7},{6,4},{7,9},{8,6},{9,11},{10,8},{11,... | collective-permute-start | bytes 393224 | tf_op jit(solution)/shard_map/ppermute | solution.py:444
  9.9 5.2 %collective-permute-start = (bf16[128,512]{1,0:T(8,128)(2,1)}, bf16[128,512]{1,0:T(8,128)(2,1)S(1)}, u32[]{:S(2)}, u32[]{:S(2)}) collective-permute-start(bf16[128,512]{1,0:T(8,128)(2,1)} %bitcast.17), channel_id=1, source_target_pairs={{0,1},{1,0},{2,3},{3,2},{4,5},{5,4},{6,7},{7,6},{8,9},{9,8},{10,11... | collective-permute-start | bytes 393224 | tf_op jit(solution)/shard_map/ppermute | solution.py:444
  15.2 0.0 collective-permute-done.3.refs_4_
  15.2 1.9 %collective-permute-start.7 = (bf16[128,512]{1,0:T(8,128)(2,1)S(1)}, bf16[128,512]{1,0:T(8,128)(2,1)S(1)}, u32[]{:S(2)}, u32[]{:S(2)}) collective-permute-start(bf16[128,512]{1,0:T(8,128)(2,1)S(1)} %collective-permute-done.3.refs_4_), channel_id=1, source_target_pairs={{3,1},{5,3},{7,5},{9,7},{11,9},{13,11},{15,13},{17,15},{19,17},{21... | collective-permute-start | bytes 393224 | tf_op jit(solution)/shard_map/ppermute | solution.py:444
  17.1 0.1 collective-permute-start.4
  17.2 0.5 collective-permute-start.2
  17.7 0.1 collective-permute-start.6
  17.8 0.9 %hold.1.refs_0_ = bf16[128,512]{1,0:T(8,128)(2,1)S(1)} custom-call(bf16[128,512]{1,0:T(8,128)(2,1)} %bitcast.18), custom_call_target="tpu_custom_call" | custom-call | tf_op jit(solution)/shard_map/hold/pallas_call | solution.py:98
  18.7 0.0 copy-start.4
  18.7 0.0 copy-start.5
  19.4 1.4 %collective-permute-done.7.refs_8_ = bf16[128,512]{1,0:T(8,128)(2,1)S(1)} collective-permute-done((bf16[128,512]{1,0:T(8,128)(2,1)S(1)}, bf16[128,512]{1,0:T(8,128)(2,1)S(1)}, u32[]{:S(2)}, u32[]{:S(2)}) %collective-permute-start.7) | collective-permute-done | bytes 131104 | tf_op jit(solution)/shard_map/ppermute | solution.py:444
  20.9 1.1 %warp.1 = (bf16[8,16,640]{2,1,0:T(8,128)(2,1)S(1)}, bf16[128,512]{1,0:T(8,128)(2,1)S(1)}) custom-call(s32[1,1,1,4]{3,2,1,0:T(1,128)S(1)} %copy-done.5, s32[1,1,1,4]{3,2,1,0:T(1,128)S(1)} %copy-done.6, s32[1,1,1,4]{3,2,1,0:T(1,128)S(1)} %copy-done.7, s32[2,1,1,1,4]{4,3,2,1,0:T(1,128)S(1)} %copy-done.4, f32[1,1]{1,0:T(1,128)S(6)} %copy.13.blend, ...), custom_call_target="tpu_custom_call" | custom-call | tf_op jit(solution)/shard_map/warp/pallas_call | solution.py:170
  22.0 17.9 %all_to_all.10.got = bf16[8,16,640]{2,1,0:T(8,128)(2,1)S(1)} all-to-all(bf16[8,16,640]{2,1,0:T(8,128)(2,1)S(1)} %get-tuple-element.16), channel_id=1, replica_groups=mesh['gz'=8,'rows'=32] {'gz'}, dimensions={0} | all-to-all | bytes 327680 | tf_op jit(solution)/shard_map/all_to_all | solution.py:463
  40.0 0.8 %prior.1 = bf16[8,16,512]{2,1,0:T(8,128)(2,1)} custom-call(bf16[8,16,640]{2,1,0:T(8,128)(2,1)S(1)} %all_to_all.10.got), custom_call_target="tpu_custom_call" | custom-call | tf_op jit(solution)/shard_map/prior/pallas_call | solution.py:209
  40.8 0.0 copy-start
  40.8 0.0 copy-start.1
  40.8 0.0 copy-start.8
  40.8 0.0 copy-start.9
  40.8 3.5 %all-to-all-start.1 = ((bf16[8,16,512]{2,1,0:T(8,128)(2,1)}), bf16[8,16,512]{2,1,0:T(8,128)(2,1)S(1)}, u32[]{:S(2)}, u32[]{:S(2)}) async-start(bf16[8,16,512]{2,1,0:T(8,128)(2,1)} %prior.1), calls=%async_computation.1 | async-start | bytes 262144 | tf_op jit(solution)/shard_map/all_to_all | solution.py:465
  44.3 0.0 copy-start.2
  44.3 0.0 copy-start.3
  44.4 0.6 copy-done.2
  45.0 0.0 copy-done.3
  45.0 0.7 %weights.1 = (bf16[1024,256]{1,0:T(8,128)(2,1)S(1)}, bf16[288,256]{1,0:T(8,128)(2,1)S(1)}, bf16[2,576,256]{2,1,0:T(8,128)(2,1)S(1)}, f32[4,32,256]{2,1,0:T(8,128)S(1)}) custom-call(bf16[9,2,32]{2,1,0:T(2,128)(2,1)S(1)} %bitcast.12, bf16[9,32,32]{2,1,0:T(8,128)(2,1)S(1)} %copy-done.1, bf16[2,9,32,32]{3,2,1,0:T(8,128)(2,1)S(1)} %copy-done, ...), custom_call_target="tpu_custom_call" | custom-call | flops 20000000 | bytes 2000000 | tf_op jit(solution)/shard_map/weights/pallas_call | solution.py:71
  45.7 6.8 %all-to-all-done.1.prior = bf16[8,16,512]{2,1,0:T(8,128)(2,1)S(1)} async-done(((bf16[8,16,512]{2,1,0:T(8,128)(2,1)}), bf16[8,16,512]{2,1,0:T(8,128)(2,1)S(1)}, u32[]{:S(2)}, u32[]{:S(2)}) %all-to-all-start.1) | async-done | bytes 131104 | tf_op jit(solution)/shard_map/all_to_all | solution.py:465
  52.5 3.5 %collective-permute-start.9 = (bf16[2,16,512]{2,1,0:T(8,128)(2,1)S(1)}, bf16[2,16,512]{2,1,0:T(8,128)(2,1)S(1)}, u32[]{:S(2)}, u32[]{:S(2)}) collective-permute-start(bf16[2,16,512]{2,1,0:T(8,128)(2,1)S(1)} %pad_maximum_fusion), channel_id=1, source_target_pairs={{1,2},{2,1},{3,4},{4,3},{5,6},{6,5},{7,8},{8,7},{9,10},{10,9},{11,... | collective-permute-start | bytes 98312 | tf_op jit(solution)/shard_map/ppermute | solution.py:444
  56.0 0.7 %collective-permute-start.8 = (bf16[2,16,512]{2,1,0:T(8,128)(2,1)S(1)}, bf16[2,16,512]{2,1,0:T(8,128)(2,1)S(1)}, u32[]{:S(2)}, u32[]{:S(2)}) collective-permute-start(bf16[2,16,512]{2,1,0:T(8,128)(2,1)S(1)} %pad_maximum_fusion), channel_id=1, source_target_pairs={{0,1},{1,0},{2,3},{3,2},{4,5},{5,4},{6,7},{7,6},{8,9},{9,8},{10,11... | collective-permute-start | bytes 98312 | tf_op jit(solution)/shard_map/ppermute | solution.py:444
  56.7 3.7 %middle.1 = (bf16[32,32,256]{2,1,0:T(8,128)(2,1)S(1)}, bf16[2,2,128,256]{3,2,1,0:T(8,128)(2,1)S(1)}, bf16[2,256,256]{2,1,0:T(8,128)(2,1)S(1)}, bf16[2,384,256]{2,1,0:T(8,128)(2,1)S(1)}) custom-call(bf16[128,512]{1,0:T(8,128)(2,1)S(1)} %get-tuple-element.15.enc, bf16[8,16,512]{2,1,0:T(8,128)(2,1)S(1)} %all-to-all-done.1.prior, ...), custom_call_target="tpu_custom_call" | custom-call | flops 6000000000 | bytes 4000000 | tf_op jit(solution)/shard_map/middle/pallas_call | solution.py:321
  60.4 2.8 %border.1 = bf16[1,1,32,64,256]{4,3,2,1,0:T(8,128)(2,1)} custom-call(bf16[128,512]{1,0:T(8,128)(2,1)S(1)} %get-tuple-element.15.enc, bf16[8,16,512]{2,1,0:T(8,128)(2,1)S(1)} %all-to-all-done.1.prior, bf16[2,16,512]{2,1,0:T(8,128)(2,1)S(1)} %collective-permute-done.8.inner, bf16[2,16,512]{2,1,0:T(8,128)(2,1)S(1)} %collective-permute-done.9.outer, ...), custom_call_target="tpu_custom_call" | custom-call | tf_op jit(solution)/shard_map/border/pallas_call | solution.py:408
  (21 shorter events, 0.1 us)
Async XLA Ops:
  0.0 8.0 %collective-permute-start.1 = (bf16[128,512]{1,0:T(8,128)(2,1)}, bf16[128,512]{1,0:T(8,128)(2,1)S(1)}, u32[]{:S(2)}, u32[]{:S(2)}) collective-permute-start(bf16[128,512]{1,0:T(8,128)(2,1)} %bitcast.15), channel_id=1, source_target_pairs={{1,3},{2,0},{3,5},{4,2},{5,7},{6,4},{7,9},{8,6},{9,11},{10,8},{11,... | collective-permute-start | bytes 393224 | tf_op jit(solution)/shard_map/ppermute | solution.py:444
  3.2 12.0 %collective-permute-start.3 = (bf16[128,512]{1,0:T(8,128)(2,1)}, bf16[128,512]{1,0:T(8,128)(2,1)S(1)}, u32[]{:S(2)}, u32[]{:S(2)}) collective-permute-start(bf16[128,512]{1,0:T(8,128)(2,1)} %bitcast.16), channel_id=1, source_target_pairs={{0,2},{2,4},{3,1},{4,6},{5,3},{6,8},{7,5},{8,10},{9,7},{10,12},{11... | collective-permute-start | bytes 393224 | tf_op jit(solution)/shard_map/ppermute | solution.py:444
  8.0 9.7 %collective-permute-start.5 = (bf16[128,512]{1,0:T(8,128)(2,1)S(1)}, bf16[128,512]{1,0:T(8,128)(2,1)S(1)}, u32[]{:S(2)}, u32[]{:S(2)}) collective-permute-start(bf16[128,512]{1,0:T(8,128)(2,1)S(1)} %collective-permute-done.1.refs_2_), channel_id=1, source_target_pairs={{1,3},{2,0},{3,5},{4,2},{5,7},{6,4},{7,9},{8,6},{9,11},{10,8},{11,... | collective-permute-start | bytes 393224 | tf_op jit(solution)/shard_map/ppermute | solution.py:444
  9.9 9.5 %collective-permute-start = (bf16[128,512]{1,0:T(8,128)(2,1)}, bf16[128,512]{1,0:T(8,128)(2,1)S(1)}, u32[]{:S(2)}, u32[]{:S(2)}) collective-permute-start(bf16[128,512]{1,0:T(8,128)(2,1)} %bitcast.17), channel_id=1, source_target_pairs={{0,1},{1,0},{2,3},{3,2},{4,5},{5,4},{6,7},{7,6},{8,9},{9,8},{10,11... | collective-permute-start | bytes 393224 | tf_op jit(solution)/shard_map/ppermute | solution.py:444
  15.2 5.7 %collective-permute-start.7 = (bf16[128,512]{1,0:T(8,128)(2,1)S(1)}, bf16[128,512]{1,0:T(8,128)(2,1)S(1)}, u32[]{:S(2)}, u32[]{:S(2)}) collective-permute-start(bf16[128,512]{1,0:T(8,128)(2,1)S(1)} %collective-permute-done.3.refs_4_), channel_id=1, source_target_pairs={{3,1},{5,3},{7,5},{9,7},{11,9},{13,11},{15,13},{17,15},{19,17},{21... | collective-permute-start | bytes 393224 | tf_op jit(solution)/shard_map/ppermute | solution.py:444
  17.1 3.8 %collective-permute-start.4 = (bf16[128,512]{1,0:T(8,128)(2,1)S(1)}, bf16[128,512]{1,0:T(8,128)(2,1)S(1)}, u32[]{:S(2)}, u32[]{:S(2)}) collective-permute-start(bf16[128,512]{1,0:T(8,128)(2,1)S(1)} %collective-permute-done.3.refs_4_), channel_id=1, source_target_pairs={{0,1},{1,0},{2,3},{3,2},{4,5},{5,4},{6,7},{7,6},{8,9},{9,8},{10,11... | collective-permute-start | bytes 393224 | tf_op jit(solution)/shard_map/ppermute | solution.py:444
  17.2 3.7 %collective-permute-start.2 = (bf16[128,512]{1,0:T(8,128)(2,1)S(1)}, bf16[128,512]{1,0:T(8,128)(2,1)S(1)}, u32[]{:S(2)}, u32[]{:S(2)}) collective-permute-start(bf16[128,512]{1,0:T(8,128)(2,1)S(1)} %collective-permute-done.1.refs_2_), channel_id=1, source_target_pairs={{0,1},{1,0},{2,3},{3,2},{4,5},{5,4},{6,7},{7,6},{8,9},{9,8},{10,11... | collective-permute-start | bytes 393224 | tf_op jit(solution)/shard_map/ppermute | solution.py:444
  17.7 3.2 %collective-permute-start.6 = (bf16[128,512]{1,0:T(8,128)(2,1)S(1)}, bf16[128,512]{1,0:T(8,128)(2,1)S(1)}, u32[]{:S(2)}, u32[]{:S(2)}) collective-permute-start(bf16[128,512]{1,0:T(8,128)(2,1)S(1)} %collective-permute-done.5.refs_6_), channel_id=1, source_target_pairs={{0,1},{1,0},{2,3},{3,2},{4,5},{5,4},{6,7},{7,6},{8,9},{9,8},{10,11... | collective-permute-start | bytes 393224 | tf_op jit(solution)/shard_map/ppermute | solution.py:444
  17.8 3.1 %copy-start.6 = (s32[1,1,1,4]{3,2,1,0:T(1,128)S(1)}, s32[1,1,1,4]{3,2,1,0:T(1,128)}, u32[]{:S(2)}) copy-start(s32[1,1,1,4]{3,2,1,0:T(1,128)} %base.1) | copy-start | bytes 52
  17.8 3.1 %copy-start.7 = (s32[1,1,1,4]{3,2,1,0:T(1,128)S(1)}, s32[1,1,1,4]{3,2,1,0:T(1,128)}, u32[]{:S(2)}) copy-start(s32[1,1,1,4]{3,2,1,0:T(1,128)} %cols.1) | copy-start | bytes 52
  18.7 2.2 %copy-start.4 = (s32[2,1,1,1,4]{4,3,2,1,0:T(1,128)S(1)}, s32[2,1,1,1,4]{4,3,2,1,0:T(1,128)}, u32[]{:S(2)}) copy-start(s32[2,1,1,1,4]{4,3,2,1,0:T(1,128)} %frac.1) | copy-start | bytes 100
  18.7 2.2 %copy-start.5 = (s32[1,1,1,4]{3,2,1,0:T(1,128)S(1)}, s32[1,1,1,4]{3,2,1,0:T(1,128)}, u32[]{:S(2)}) copy-start(s32[1,1,1,4]{3,2,1,0:T(1,128)} %offs.1) | copy-start | bytes 52
  40.8 3.6 %copy-start = (bf16[2,9,32,32]{3,2,1,0:T(8,128)(2,1)S(1)}, bf16[2,9,32,32]{3,2,1,0:T(8,128)(2,1)}, u32[]{:S(2)}) copy-start(bf16[2,9,32,32]{3,2,1,0:T(8,128)(2,1)} %kp.1) | copy-start | bytes 110596
  40.8 3.6 %copy-start.1 = (bf16[9,32,32]{2,1,0:T(8,128)(2,1)S(1)}, bf16[9,32,32]{2,1,0:T(8,128)(2,1)}, u32[]{:S(2)}) copy-start(bf16[9,32,32]{2,1,0:T(8,128)(2,1)} %kd.1) | copy-start | bytes 55300
  40.8 3.6 %copy-start.8 = (f32[32]{0:T(128)S(1)}, f32[32]{0:T(128)}, u32[]{:S(2)}) copy-start(f32[32]{0:T(128)} %param.19) | copy-start | bytes 388
  40.8 3.6 %copy-start.9 = (f32[32]{0:T(128)S(1)}, f32[32]{0:T(128)}, u32[]{:S(2)}) copy-start(f32[32]{0:T(128)} %param.21) | copy-start | bytes 388
  40.8 11.7 %all-to-all-start.1 = ((bf16[8,16,512]{2,1,0:T(8,128)(2,1)}), bf16[8,16,512]{2,1,0:T(8,128)(2,1)S(1)}, u32[]{:S(2)}, u32[]{:S(2)}) async-start(bf16[8,16,512]{2,1,0:T(8,128)(2,1)} %prior.1), calls=%async_computation.1 | async-start | bytes 262144 | tf_op jit(solution)/shard_map/all_to_all | solution.py:465
  44.3 0.7 %copy-start.2 = (bf16[9,32,2]{1,2,0:T(2,128)(2,1)S(1)}, bf16[9,32,2]{1,2,0:T(2,128)(2,1)}, u32[]{:S(2)}) copy-start(bf16[9,32,2]{1,2,0:T(2,128)(2,1)} %param.18) | copy-start | bytes 3460
  44.3 0.7 %copy-start.3 = (f32[2,32]{1,0:T(2,128)S(1)}, f32[2,32]{1,0:T(2,128)}, u32[]{:S(2)}) copy-start(f32[2,32]{1,0:T(2,128)} %bp.1) | copy-start | bytes 772
  52.5 7.9 %collective-permute-start.9 = (bf16[2,16,512]{2,1,0:T(8,128)(2,1)S(1)}, bf16[2,16,512]{2,1,0:T(8,128)(2,1)S(1)}, u32[]{:S(2)}, u32[]{:S(2)}) collective-permute-start(bf16[2,16,512]{2,1,0:T(8,128)(2,1)S(1)} %pad_maximum_fusion), channel_id=1, source_target_pairs={{1,2},{2,1},{3,4},{4,3},{5,6},{6,5},{7,8},{8,7},{9,10},{10,9},{11,... | collective-permute-start | bytes 98312 | tf_op jit(solution)/shard_map/ppermute | solution.py:444
  56.0 4.4 %collective-permute-start.8 = (bf16[2,16,512]{2,1,0:T(8,128)(2,1)S(1)}, bf16[2,16,512]{2,1,0:T(8,128)(2,1)S(1)}, u32[]{:S(2)}, u32[]{:S(2)}) collective-permute-start(bf16[2,16,512]{2,1,0:T(8,128)(2,1)S(1)} %pad_maximum_fusion), channel_id=1, source_target_pairs={{0,1},{1,0},{2,3},{3,2},{4,5},{5,4},{6,7},{7,6},{8,9},{9,8},{10,11... | collective-permute-start | bytes 98312 | tf_op jit(solution)/shard_map/ppermute | solution.py:444
